TPU v7x, 32 devices: a whole 2x2x4 slice. The times are simulated.
32 devices in a mesh: dp: 8 (over y, x, core), mp: 4 (over z).
Axes of the slice: x: 2, y: 2, z: 4, core: 2. Of those that a mesh axis runs over, the one named last changes fastest.
Arguments:
- tokens: bfloat16 [16384, 768], P(('dp', 'mp')), may hold values from -6 to 6
- segments: int32 [32, 512], P('dp'), may hold values from 0 to 5, never falling along the last dimension, each value on 1 to 256 neighbouring positions
- w_query: bfloat16 [768, 768], P(None, 'mp'), may hold values from -0.21875 to 0.21875
- b_query: bfloat16 [768], P('mp'), may hold values from -3 to 3
- w_key: bfloat16 [768, 768], P(None, 'mp'), may hold values from -0.21875 to 0.21875
- w_value: bfloat16 [768, 768], P(None, 'mp'), may hold values from -0.21875 to 0.21875
- b_value: bfloat16 [768], P('mp'), may hold values from -3 to 3
- w_out: bfloat16 [768, 768], P('mp'), may hold values from -0.625 to 0.625
- b_out: bfloat16 [768], replicated, may hold values from -3 to 3
- first_norm_gain: bfloat16 [768], replicated, may hold values from 0.099609375 to 1.8984375
- first_norm_bias: bfloat16 [768], replicated, may hold values from -3 to 3
- w_up: bfloat16 [768, 3072], P(None, 'mp'), may hold values from -0.21875 to 0.21875
- b_up: bfloat16 [3072], P('mp'), may hold values from -3 to 3
- w_down: bfloat16 [3072, 768], P('mp'), may hold values from -0.109375 to 0.109375
- b_down: bfloat16 [768], replicated, may hold values from -3 to 3
- second_norm_gain: bfloat16 [768], replicated, may hold values from 0.099609375 to 1.8984375
- second_norm_bias: bfloat16 [768], replicated, may hold values from -3 to 3
- output_gradient: bfloat16 [16384, 768], P(('dp', 'mp')), may hold values from -6 to 6
Outputs:
- out_tokens: bfloat16 [16384, 768], P(('dp', 'mp'))
- grad_tokens: bfloat16 [16384, 768], P(('dp', 'mp'))
- grad_w_query: float32 [768, 768], P(None, 'mp')
- grad_b_query: float32 [768], P('mp')
- grad_w_key: float32 [768, 768], P(None, 'mp')
- grad_w_value: float32 [768, 768], P(None, 'mp')
- grad_b_value: float32 [768], P('mp')
- grad_w_out: float32 [768, 768], P('mp')
- grad_b_out: float32 [768], replicated
- grad_norm1_gain: float32 [768], replicated
- grad_norm1_bias: float32 [768], replicated
- grad_w_up: float32 [768, 3072], P(None, 'mp')
- grad_b_up: float32 [3072], P('mp')
- grad_w_down: float32 [3072, 768], P('mp')
- grad_b_down: float32 [768], replicated
- grad_norm2_gain: float32 [768], replicated
- grad_norm2_bias: float32 [768], replicated
Inputs may be any that keep to these rules, and one draw needn't show every extreme that they name: `segments`: document numbers never fall along a sequence; a document holds 1 to 256 positions, and in every sequence one holds exactly 256.
All inputs are finite; a program needn't handle non-finite values.
Results may differ from a plain program's by a relative error of at most 0.015.
Values may be sent and summed in bfloat16 or wider, within the bound.
No kernel may reach another device: no remote copies, remote signals or barrier semaphores. Data moves between devices by JAX's collectives and lax.ppermute only.
A program may use at most 128 MiB of HBM per device.

v0:
```python
import jax
import jax.numpy as jnp
from jax import lax
from jax.sharding import PartitionSpec as P

HEAD_DIM = 64
EPS = 1e-05
INV_ROOT_TWO = 0.7071067811865476
INV_ROOT_TWO_PI = 0.3989422804014327
CUBE = 8
f32 = jnp.float32
bf16 = jnp.bfloat16


def dot(left, right, dims):
    return lax.dot_general(
        left, right, ((dims[:1], dims[1:]), ((), ())), preferred_element_type=f32
    )


def norm_forward(values, gain, bias):
    average = jnp.mean(values, -1, keepdims=True)
    centered = values - average
    spread = jnp.mean(centered * centered, -1, keepdims=True)
    rstd = lax.rsqrt(spread + EPS)
    xhat = centered * rstd
    return (xhat * gain + bias, xhat, rstd)


def norm_backward(grad, xhat, rstd, gain):
    scaled = grad * gain
    result = rstd * (
        scaled
        - jnp.mean(scaled, -1, keepdims=True)
        - xhat * jnp.mean(scaled * xhat, -1, keepdims=True)
    )
    return (result, jnp.sum(grad * xhat, 0), jnp.sum(grad, 0))


def gelu_parts(v):
    phi = 0.5 * (1.0 + lax.erf(v * INV_ROOT_TWO))
    return (v * phi, phi + v * jnp.exp(-0.5 * v * v) * INV_ROOT_TWO_PI)


class Links:

    def __init__(self, dp, mp):
        self.dp, self.mp = (dp, mp)
        self.index = lax.axis_index("dp")
        self.place = self.index % CUBE

    def shift(self, x, by):
        return lax.ppermute(x, "mp", [(i, (i + by) % self.mp) for i in range(self.mp)])

    def flip(self, x, bit):
        return lax.ppermute(x, "dp", [(i, i ^ bit) for i in range(self.dp)])

    def spread(self, piece):
        half = piece.shape[0] // 2
        over_x = self.flip(piece, 2)
        over_y = self.flip(piece, 4)
        diag_a = self.flip(over_x[:half], 4)
        diag_b = self.flip(over_y[half:], 2)
        diag = jnp.concatenate([diag_a, diag_b])
        even = [piece, over_x, over_y, diag]
        odd = [self.flip(part, 1) for part in even]
        return [even[0], odd[0], even[1], odd[1], even[2], odd[2], even[3], odd[3]]

    def ordered(self, parts):
        stacked = jnp.stack(parts)
        return jnp.stack(
            [
                lax.dynamic_index_in_dim(stacked, self.place ^ q, 0, keepdims=False)
                for q in range(CUBE)
            ]
        )

    def gather(self, shard):
        rows, cols = shard.shape
        step = rows // CUBE
        piece = lax.dynamic_slice_in_dim(shard, self.place * step, step, 0)
        others = jnp.concatenate([self.shift(piece, s) for s in range(1, self.mp)])
        whole = self.ordered(self.spread(others)).reshape(CUBE, self.mp - 1, step, cols)
        whole = whole.transpose(1, 0, 2, 3).reshape(self.mp - 1, rows, cols)
        return [shard] + [whole[s] for s in range(self.mp - 1)]

    def reduce(self, blocks):
        rows, cols = blocks[0].shape
        step = rows // CUBE
        stacked = jnp.stack(blocks).reshape(self.mp, CUBE, step, cols)
        rel = [
            lax.dynamic_index_in_dim(stacked, self.place ^ r, 1, keepdims=False).astype(bf16)
            for r in range(CUBE)
        ]
        other = self.flip(jnp.stack(rel[1::2]), 1)
        add = lambda *terms: sum((t.astype(f32) for t in terms)).astype(bf16)
        own, to_x, to_y, to_diag = [add(rel[2 * i], other[i]) for i in range(4)]
        cut = self.mp // 2
        a, b = (slice(0, cut), slice(cut, self.mp))
        from_x = self.flip(jnp.stack([to_diag[a], to_x[a]]), 2)
        from_y = self.flip(jnp.stack([to_diag[b], to_y[b]]), 4)
        last_x = self.flip(add(to_x[b], from_y[0]), 2)
        last_y = self.flip(add(to_y[a], from_x[0]), 4)
        own = jnp.concatenate([add(own[a], from_x[1], last_y), add(own[b], last_x, from_y[1])])
        terms = [own[0]] + [self.shift(own[s], -s) for s in range(1, self.mp)]
        total = sum((t.astype(f32) for t in terms))
        if self.dp > CUBE:
            groups = [[g * CUBE + i for g in range(self.dp // CUBE)] for i in range(CUBE)]
            total = lax.psum(total, "dp", axis_index_groups=groups)
        return total


def scores_of(queries, key_rows, same_doc):
    scores = jnp.einsum("qhd,khd->hqk", queries, key_rows, preferred_element_type=f32)
    return jnp.where(same_doc[None], scores * HEAD_DIM ** (-0.5), -1e30)


def attend_forward(queries, key_rows, value_rows, same_doc):
    scores = scores_of(queries, key_rows, same_doc)
    highest = jnp.max(scores, -1, keepdims=True)
    expd = jnp.exp(scores - highest)
    totals = jnp.sum(expd, -1, keepdims=True)
    probs = (expd / totals).astype(bf16)
    context = jnp.einsum("hqk,khd->qhd", probs, value_rows, preferred_element_type=f32)
    return (context.astype(bf16), (highest + jnp.log(totals))[..., 0])


def attend_backward(queries, key_rows, value_rows, g_context, log_sums, same_doc):
    scores = scores_of(queries, key_rows, same_doc)
    probs = jnp.exp(scores - log_sums[..., None])
    g_value = jnp.einsum("hqk,qhd->khd", probs.astype(bf16), g_context, preferred_element_type=f32)
    g_probs = jnp.einsum("qhd,khd->hqk", g_context, value_rows, preferred_element_type=f32)
    centre = jnp.sum(probs * g_probs, -1, keepdims=True)
    g_scores = (probs * (g_probs - centre)).astype(bf16)
    scale = HEAD_DIM ** (-0.5)
    g_query = scale * jnp.einsum("hqk,khd->qhd", g_scores, key_rows, preferred_element_type=f32)
    g_key = scale * jnp.einsum("hqk,qhd->khd", g_scores, queries, preferred_element_type=f32)
    return (g_query.astype(bf16), g_key.astype(bf16), g_value.astype(bf16))


def per_device(
    dp,
    mp,
    tokens,
    segments,
    w_query,
    b_query,
    w_key,
    w_value,
    b_value,
    w_out,
    b_out,
    first_norm_gain,
    first_norm_bias,
    w_up,
    b_up,
    w_down,
    b_down,
    second_norm_gain,
    second_norm_bias,
    output_gradient,
):
    links = Links(dp, mp)
    slots = range(mp)
    rows, width = tokens.shape
    part = w_query.shape[1]
    heads = part // HEAD_DIM
    gain1, bias1 = (first_norm_gain.astype(f32), first_norm_bias.astype(f32))
    gain2, bias2 = (second_norm_gain.astype(f32), second_norm_bias.astype(f32))
    segment = lax.dynamic_index_in_dim(segments, lax.axis_index("mp"), 0, keepdims=False)
    same_doc = segment[:, None] == segment[None, :]
    mixed = jnp.concatenate([w_query, w_key, w_value, w_out.T], axis=1)
    a_blocks = links.gather(mixed)
    vectors = jnp.concatenate([b_query, b_value, b_up])
    vectors = [vectors] + [links.shift(vectors, s) for s in range(1, mp)]
    bq = [v[:part].astype(f32) for v in vectors]
    bv = [v[part : 2 * part].astype(f32) for v in vectors]
    bu = [v[2 * part :].astype(f32) for v in vectors]
    u_blocks = links.gather(w_up)
    d_blocks = links.gather(w_down)
    by_head = lambda t: t.reshape(rows, heads, HEAD_DIM)
    by_rows = lambda t: t.reshape(rows, heads * HEAD_DIM)
    saved = []
    attended = tokens.astype(f32) + b_out.astype(f32)
    for s in slots:
        mix = dot(tokens, a_blocks[s][:, : 3 * part], (1, 0))
        q = by_head((mix[:, :part] + bq[s]).astype(bf16))
        k = by_head(mix[:, part : 2 * part].astype(bf16))
        v = by_head((mix[:, 2 * part :] + bv[s]).astype(bf16))
        context, sums = attend_forward(q, k, v, same_doc)
        context = by_rows(context)
        saved.append((q, k, v, context, sums))
        attended = attended + dot(context, a_blocks[s][:, 3 * part :], (1, 1))
    normed, xhat1, rstd1 = norm_forward(attended, gain1, bias1)
    normed_low = normed.astype(bf16)
    acts, slopes = ([], [])
    summed = normed + b_down.astype(f32)
    for s in slots:
        act, slope = gelu_parts(dot(normed_low, u_blocks[s], (1, 0)) + bu[s])
        acts.append(act.astype(bf16))
        slopes.append(slope)
        summed = summed + dot(acts[s], d_blocks[s], (1, 0))
    out_tokens, xhat2, rstd2 = norm_forward(summed, gain2, bias2)
    g_summed, g_gain2, g_bias2 = norm_backward(output_gradient.astype(f32), xhat2, rstd2, gain2)
    g_b_down = jnp.sum(g_summed, 0)
    g_low = g_summed.astype(bf16)
    piece_d = links.reduce([dot(acts[s], g_low, (0, 0)) for s in slots])
    g_pre = [(dot(g_low, d_blocks[s], (1, 1)) * slopes[s]).astype(bf16) for s in slots]
    piece_u = links.reduce([dot(normed_low, g_pre[s], (0, 0)) for s in slots])
    g_b_up = [jnp.sum(g.astype(f32), 0) for g in g_pre]
    g_normed = g_summed
    for s in slots:
        g_normed = g_normed + dot(g_pre[s], u_blocks[s], (1, 1))
    g_attended, g_gain1, g_bias1 = norm_backward(g_normed, xhat1, rstd1, gain1)
    g_b_out = jnp.sum(g_attended, 0)
    ga_low = g_attended.astype(bf16)
    g_tokens = g_attended
    g_mixed, g_bq, g_bv = ([], [], [])
    for s in slots:
        q, k, v, context, sums = saved[s]
        g_out = dot(ga_low, context, (0, 0))
        g_context = by_head(dot(ga_low, a_blocks[s][:, 3 * part :], (1, 0)).astype(bf16))
        gq, gk, gv = attend_backward(q, k, v, g_context, sums, same_doc)
        gq, gk, gv = (by_rows(gq), by_rows(gk), by_rows(gv))
        g_bq.append(jnp.sum(gq.astype(f32), 0))
        g_bv.append(jnp.sum(gv.astype(f32), 0))
        g_qkv = jnp.concatenate([gq, gk, gv], axis=1)
        g_tokens = g_tokens + dot(g_qkv, a_blocks[s][:, : 3 * part], (1, 1))
        g_mixed.append(jnp.concatenate([dot(tokens, g_qkv, (0, 0)), g_out], axis=1))
    piece_a = links.reduce(g_mixed)
    pieces = jnp.concatenate([piece_a, piece_u, piece_d]).astype(bf16)
    step = width // CUBE
    whole = links.ordered(links.spread(pieces)).reshape(CUBE, 3, step, width)
    whole = whole.transpose(1, 0, 2, 3).reshape(3, width, width).astype(f32)
    g_a, g_u, g_d = (whole[0], whole[1], whole[2])
    shared = jnp.stack([g_gain1, g_bias1, g_b_out, g_gain2, g_bias2, g_b_down])
    shared = lax.psum(shared, ("dp", "mp"))
    split = [jnp.concatenate([g_bq[s], g_bv[s], g_b_up[s]]) for s in slots]
    mine = split[0] + sum((links.shift(split[s], -s) for s in range(1, mp)))
    mine = lax.psum(mine, "dp")
    return (
        out_tokens.astype(bf16),
        g_tokens.astype(bf16),
        g_a[:, :part],
        mine[:part],
        g_a[:, part : 2 * part],
        g_a[:, 2 * part : 3 * part],
        mine[part : 2 * part],
        g_a[:, 3 * part :].T,
        shared[2],
        shared[0],
        shared[1],
        g_u,
        mine[2 * part :],
        g_d,
        shared[5],
        shared[3],
        shared[4],
    )


def solution(mesh):
    rows, cols = (P(("dp", "mp"), None), P(None, "mp"))
    in_specs = (
        rows,
        P("dp", None),
        cols,
        P("mp"),
        cols,
        cols,
        P("mp"),
        P("mp", None),
        P(),
        P(),
        P(),
        cols,
        P("mp"),
        P("mp", None),
        P(),
        P(),
        P(),
        rows,
    )
    out_specs = (
        rows,
        rows,
        cols,
        P("mp"),
        cols,
        cols,
        P("mp"),
        P("mp", None),
        P(),
        P(),
        P(),
        cols,
        P("mp"),
        P("mp", None),
        P(),
        P(),
        P(),
    )
    dp, mp = (mesh.shape["dp"], mesh.shape["mp"])

    def step(*args):
        return per_device(dp, mp, *args)

    return jax.shard_map(step, mesh=mesh, in_specs=in_specs, out_specs=out_specs, check_vma=False)
```

profile of v0, /device:TPU:0, one launch (start us, length us, event | category | flops | bytes accessed | tf_op | source)
XLA Modules:
  0.0 417.6 jit_solution(2598088407525156642)
XLA Ops:
  2.4 3.0 collective-permute-start.25
  5.5 2.6 collective-permute-start.26
  9.4 2.1 concatenate.93
  31.6 3.6 collective-permute-done.11
  39.1 3.0 collective-permute-start.15
  44.5 3.0 collective-permute-done.14
  51.8 4.2 %collective-permute-done.15 = bf16[96,768]{1,0:T(8,128)(2,1)S(1)} collective-permute-done((bf16[96,768]{1,0:T(8,128)(2,1)S(1)}, bf16[96,768]{1,0:T(8,128)(2,1)S(1)}, u32[]{:S(2)}, u32[]{:S(2)}) %collective-permute-start.15) | collective-permute-done | bytes 147488 | tf_op jit(solution)/shard_map/ppermute | solution.py:53
  59.2 2.6 collective-permute-done.29
  63.4 6.3 %collective-permute-done.4 = bf16[288,768]{1,0:T(8,128)(2,1)S(1)} collective-permute-done((bf16[288,768]{1,0:T(8,128)(2,1)S(1)}, bf16[288,768]{1,0:T(8,128)(2,1)S(1)}, u32[]{:S(2)}, u32[]{:S(2)}) %collective-permute-start.4) | collective-permute-done | bytes 442400 | tf_op jit(solution)/shard_map/ppermute | solution.py:56
  75.7 7.0 %collective-permute-done.18 = bf16[288,768]{1,0:T(8,128)(2,1)S(1)} collective-permute-done((bf16[288,768]{1,0:T(8,128)(2,1)S(1)}, bf16[288,768]{1,0:T(8,128)(2,1)S(1)}, u32[]{:S(2)}, u32[]{:S(2)}) %collective-permute-start.18) | collective-permute-done | bytes 442400 | tf_op jit(solution)/shard_map/ppermute | solution.py:56
  85.9 3.2 collective-permute-done.33
  89.6 3.7 collective-permute-done.8
  93.4 2.3 collective-permute-done.22
  116.2 2.0 multiply_convert_fusion.7
  126.7 2.1 fusion.177
  178.9 2.0 copy-done.6
  183.6 2.0 copy-done.7
  193.9 2.4 copy.90
  199.2 2.4 copy.89
  204.4 2.4 copy.88
  206.8 2.3 pad_maximum_fusion
  209.3 2.0 copy-done.5
  216.0 3.2 collective-permute-start.68
  225.7 6.5 %collective-permute-start.70 = (f32[1152]{0:T(1024)S(1)}, f32[1152]{0:T(1024)S(1)}, u32[]{:S(2)}, u32[]{:S(2)}) collective-permute-start(f32[1152]{0:T(1024)S(1)} %concatenate.115), channel_id=1, source_target_pairs={{0,1},{1,2},{2,3},{3,0},{4,5},{5,6},{6,7},{7,4},{8,9},{9,10},{10,1... | collective-permute-start | bytes 13832 | tf_op jit(solution)/shard_map/ppermute | solution.py:53
  232.7 40.8 %psum.15 = f32[6,768]{1,0:T(8,128)S(1)} all-reduce(f32[6,768]{1,0:T(8,128)S(1)} %stack.372), channel_id=1, replica_groups=mesh['dp'=8,'mp'=4] {'dp','mp'}, use_global_device_ids=true, to_apply=%region_39.40 | all-reduce | flops 4608 | bytes 36864 | tf_op jit(solution)/shard_map/psum | solution.py:237
  274.2 5.6 %fusion.59 = (bf16[4,96,768]{2,1,0:T(8,128)(2,1)S(1)}, bf16[4,96,768]{2,1,0:T(8,128)(2,1)S(1)}, bf16[4,96,768]{2,1,0:T(8,128)(2,1)S(1)}, bf16[4,96,768]{2,1,0:T(...) fusion(bf16[4,8,96,768]{3,2,0,1:T(8,128)(2,1)} %copy-done.6, ...), kind=kLoop, calls=%fused_computation.155 | loop fusion | flops 9437184 | bytes 14155792 | tf_op jit(solution)/shard_map/convert_element_type | solution.py:96
  280.0 2.3 collective-permute-start.53
  284.8 2.2 fusion.67
  287.3 9.3 %collective-permute-done.53 = bf16[2,2,96,768]{3,2,1,0:T(8,128)(2,1)S(1)} collective-permute-done((bf16[2,2,96,768]{3,2,1,0:T(8,128)(2,1)S(1)}, bf16[2,2,96,768]{3,2,1,0:T(8,128)(2,1)S(1)}, u32[]{:S(2)}, u32[]{:S(2)}) %collective-permute-start.53) | collective-permute-done | bytes 589856 | tf_op jit(solution)/shard_map/ppermute | solution.py:56
  296.5 2.0 collective-permute-start.48
  300.3 8.9 %collective-permute-done.45 = bf16[2,2,96,768]{3,2,1,0:T(8,128)(2,1)S(1)} collective-permute-done((bf16[2,2,96,768]{3,2,1,0:T(8,128)(2,1)S(1)}, bf16[2,2,96,768]{3,2,1,0:T(8,128)(2,1)S(1)}, u32[]{:S(2)}, u32[]{:S(2)}) %collective-permute-start.45) | collective-permute-done | bytes 589856 | tf_op jit(solution)/shard_map/ppermute | solution.py:56
  309.2 2.0 collective-permute-start.40
  311.5 8.7 %collective-permute-done.37 = bf16[2,2,96,768]{3,2,1,0:T(8,128)(2,1)S(1)} collective-permute-done((bf16[2,2,96,768]{3,2,1,0:T(8,128)(2,1)S(1)}, bf16[2,2,96,768]{3,2,1,0:T(8,128)(2,1)S(1)}, u32[]{:S(2)}, u32[]{:S(2)}) %collective-permute-start.37) | collective-permute-done | bytes 589856 | tf_op jit(solution)/shard_map/ppermute | solution.py:56
  322.0 3.5 collective-permute-done.40
  325.5 2.0 collective-permute-start.46
  327.6 4.2 %collective-permute-done.54 = bf16[2,96,768]{2,1,0:T(8,128)(2,1)S(1)} collective-permute-done((bf16[2,96,768]{2,1,0:T(8,128)(2,1)S(1)}, bf16[2,96,768]{2,1,0:T(8,128)(2,1)S(1)}, u32[]{:S(2)}, u32[]{:S(2)}) %collective-permute-start.54) | collective-permute-done | bytes 294944 | tf_op jit(solution)/shard_map/ppermute | solution.py:56
  331.8 2.0 collective-permute-start.49
  335.6 2.0 collective-permute-done.46
  340.7 2.2 collective-permute-start.58
  344.3 2.3 collective-permute-start.55
  347.8 9.6 %collective-permute-done.58 = bf16[96,768]{1,0:T(8,128)(2,1)S(1)} collective-permute-done((bf16[96,768]{1,0:T(8,128)(2,1)S(1)}, bf16[96,768]{1,0:T(8,128)(2,1)S(1)}, u32[]{:S(2)}, u32[]{:S(2)}) %collective-permute-start.58) | collective-permute-done | bytes 147488 | tf_op jit(solution)/shard_map/ppermute | solution.py:53
  358.9 5.4 %collective-permute-start.43 = (bf16[96,768]{1,0:T(8,128)(2,1)S(1)}, bf16[96,768]{1,0:T(8,128)(2,1)S(1)}, u32[]{:S(2)}, u32[]{:S(2)}) collective-permute-start(bf16[96,768]{1,0:T(8,128)(2,1)S(1)} %get-tuple-element.114), channel_id=1, source_target_pairs={{0,1},{1,2},{2,3},{3,0},{4,5},{5,6},{6,7},{7,4},{8,9},{9,10},{10,1... | collective-permute-start | bytes 442376 | tf_op jit(solution)/shard_map/ppermute | solution.py:53
  364.3 4.2 %collective-permute-done.50 = bf16[96,768]{1,0:T(8,128)(2,1)S(1)} collective-permute-done((bf16[96,768]{1,0:T(8,128)(2,1)S(1)}, bf16[96,768]{1,0:T(8,128)(2,1)S(1)}, u32[]{:S(2)}, u32[]{:S(2)}) %collective-permute-start.50) | collective-permute-done | bytes 147488 | tf_op jit(solution)/shard_map/ppermute | solution.py:53
  368.5 3.4 collective-permute-done.47
  372.3 2.5 collective-permute-start.69
  379.2 18.9 %psum.14 = f32[1152]{0:T(1024)S(1)} all-reduce(f32[1152]{0:T(1024)S(1)} %add_add_fusion.3), channel_id=1, replica_groups=mesh['dp'=8,'mp'=4] {'dp'}, use_global_device_ids=true, to_apply=%region_32.33 | all-reduce | flops 1152 | bytes 9216 | tf_op jit(solution)/shard_map/psum | solution.py:240
  400.5 4.9 %collective-permute-done.65 = bf16[144,768]{1,0:T(8,128)(2,1)S(1)} collective-permute-done((bf16[144,768]{1,0:T(8,128)(2,1)S(1)}, bf16[144,768]{1,0:T(8,128)(2,1)S(1)}, u32[]{:S(2)}, u32[]{:S(2)}) %collective-permute-start.65) | collective-permute-done | bytes 221216 | tf_op jit(solution)/shard_map/ppermute | solution.py:56
  409.9 2.7 fusion.180
  (561 shorter events, 186.7 us)
Async XLA Ops:
  2.4 32.8 %collective-permute-start.25 = (bf16[96,768]{1,0:T(8,128)(2,1)}, bf16[96,768]{1,0:T(8,128)(2,1)}, u32[]{:S(2)}, u32[]{:S(2)}) collective-permute-start(bf16[96,768]{1,0:T(8,128)(2,1)} %constant_dynamic-slice_fusion), channel_id=1, source_target_pairs={{0,1},{1,2},{2,3},{3,0},{4,5},{5,6},{6,7},{7,4},{8,9},{9,10},{10,1... | collective-permute-start | bytes 442376 | tf_op jit(solution)/shard_map/ppermute | solution.py:53
  5.5 31.1 %collective-permute-start.26 = (bf16[96,768]{1,0:T(8,128)(2,1)}, bf16[96,768]{1,0:T(8,128)(2,1)}, u32[]{:S(2)}, u32[]{:S(2)}) collective-permute-start(bf16[96,768]{1,0:T(8,128)(2,1)} %constant_dynamic-slice_fusion), channel_id=1, source_target_pairs={{0,2},{1,3},{2,0},{3,1},{4,6},{5,7},{6,4},{7,5},{8,10},{9,11},{10,... | collective-permute-start | bytes 442376 | tf_op jit(solution)/shard_map/ppermute | solution.py:53
  8.1 31.1 %collective-permute-start.27 = (bf16[96,768]{1,0:T(8,128)(2,1)}, bf16[96,768]{1,0:T(8,128)(2,1)}, u32[]{:S(2)}, u32[]{:S(2)}) collective-permute-start(bf16[96,768]{1,0:T(8,128)(2,1)} %constant_dynamic-slice_fusion), channel_id=1, source_target_pairs={{0,3},{1,0},{2,1},{3,2},{4,7},{5,4},{6,5},{7,6},{8,11},{9,8},{10,9... | collective-permute-start | bytes 442376 | tf_op jit(solution)/shard_map/ppermute | solution.py:53
  11.5 18.0 %collective-permute-start.13 = (bf16[1152]{0:T(1024)(128)(2,1)S(1)}, bf16[1152]{0:T(1024)(128)(2,1)S(1)}, u32[]{:S(2)}, u32[]{:S(2)}) collective-permute-start(bf16[1152]{0:T(1024)(128)(2,1)S(1)} %concatenate.93), channel_id=1, source_target_pairs={{0,3},{1,0},{2,1},{3,2},{4,7},{5,4},{6,5},{7,6},{8,11},{9,8},{10,9... | collective-permute-start | bytes 6920 | tf_op jit(solution)/shard_map/ppermute | solution.py:53
  11.9 17.8 %collective-permute-start.12 = (bf16[1152]{0:T(1024)(128)(2,1)S(1)}, bf16[1152]{0:T(1024)(128)(2,1)S(1)}, u32[]{:S(2)}, u32[]{:S(2)}) collective-permute-start(bf16[1152]{0:T(1024)(128)(2,1)S(1)} %concatenate.93), channel_id=1, source_target_pairs={{0,2},{1,3},{2,0},{3,1},{4,6},{5,7},{6,4},{7,5},{8,10},{9,11},{10,... | collective-permute-start | bytes 6920 | tf_op jit(solution)/shard_map/ppermute | solution.py:53
  29.7 13.4 %collective-permute-start = (bf16[96,768]{1,0:T(8,128)(2,1)S(1)}, bf16[96,768]{1,0:T(8,128)(2,1)S(1)}, u32[]{:S(2)}, u32[]{:S(2)}) collective-permute-start(bf16[96,768]{1,0:T(8,128)(2,1)S(1)} %fusion.167), channel_id=1, source_target_pairs={{0,1},{1,2},{2,3},{3,0},{4,5},{5,6},{6,7},{7,4},{8,9},{9,10},{10,1... | collective-permute-start | bytes 442376 | tf_op jit(solution)/shard_map/ppermute | solution.py:53
  35.1 13.5 %collective-permute-start.1 = (bf16[96,768]{1,0:T(8,128)(2,1)S(1)}, bf16[96,768]{1,0:T(8,128)(2,1)S(1)}, u32[]{:S(2)}, u32[]{:S(2)}) collective-permute-start(bf16[96,768]{1,0:T(8,128)(2,1)S(1)} %fusion.167), channel_id=1, source_target_pairs={{0,2},{1,3},{2,0},{3,1},{4,6},{5,7},{6,4},{7,5},{8,10},{9,11},{10,... | collective-permute-start | bytes 442376 | tf_op jit(solution)/shard_map/ppermute | solution.py:53
  35.2 15.0 %collective-permute-start.2 = (bf16[96,768]{1,0:T(8,128)(2,1)S(1)}, bf16[96,768]{1,0:T(8,128)(2,1)S(1)}, u32[]{:S(2)}, u32[]{:S(2)}) collective-permute-start(bf16[96,768]{1,0:T(8,128)(2,1)S(1)} %fusion.167), channel_id=1, source_target_pairs={{0,3},{1,0},{2,1},{3,2},{4,7},{5,4},{6,5},{7,6},{8,11},{9,8},{10,9... | collective-permute-start | bytes 442376 | tf_op jit(solution)/shard_map/ppermute | solution.py:53
  36.6 10.9 %collective-permute-start.14 = (bf16[96,768]{1,0:T(8,128)(2,1)S(1)}, bf16[96,768]{1,0:T(8,128)(2,1)S(1)}, u32[]{:S(2)}, u32[]{:S(2)}) collective-permute-start(bf16[96,768]{1,0:T(8,128)(2,1)S(1)} %constant_dynamic-slice_fusion.1), channel_id=1, source_target_pairs={{0,1},{1,2},{2,3},{3,0},{4,5},{5,6},{6,7},{7,4},{8,9},{9,10},{10,1... | collective-permute-start | bytes 442376 | tf_op jit(solution)/shard_map/ppermute | solution.py:53
  39.1 16.8 %collective-permute-start.15 = (bf16[96,768]{1,0:T(8,128)(2,1)S(1)}, bf16[96,768]{1,0:T(8,128)(2,1)S(1)}, u32[]{:S(2)}, u32[]{:S(2)}) collective-permute-start(bf16[96,768]{1,0:T(8,128)(2,1)S(1)} %constant_dynamic-slice_fusion.1), channel_id=1, source_target_pairs={{0,2},{1,3},{2,0},{3,1},{4,6},{5,7},{6,4},{7,5},{8,10},{9,11},{10,... | collective-permute-start | bytes 442376 | tf_op jit(solution)/shard_map/ppermute | solution.py:53
  43.1 14.4 %collective-permute-start.16 = (bf16[96,768]{1,0:T(8,128)(2,1)S(1)}, bf16[96,768]{1,0:T(8,128)(2,1)S(1)}, u32[]{:S(2)}, u32[]{:S(2)}) collective-permute-start(bf16[96,768]{1,0:T(8,128)(2,1)S(1)} %constant_dynamic-slice_fusion.1), channel_id=1, source_target_pairs={{0,3},{1,0},{2,1},{3,2},{4,7},{5,4},{6,5},{7,6},{8,11},{9,8},{10,9... | collective-permute-start | bytes 442376 | tf_op jit(solution)/shard_map/ppermute | solution.py:53
  47.5 25.3 %collective-permute-start.28 = (bf16[288,768]{1,0:T(8,128)(2,1)S(1)}, bf16[288,768]{1,0:T(8,128)(2,1)S(1)}, u32[]{:S(2)}, u32[]{:S(2)}) collective-permute-start(bf16[288,768]{1,0:T(8,128)(2,1)S(1)} %constant_dynamic-update-slice_fusion.13), channel_id=1, source_target_pairs={{0,4},{4,0},{8,12},{12,8},{16,20},{20,16},{24,28},{28,24},{1,5},{5... | collective-permute-start | bytes 1327112 | tf_op jit(solution)/shard_map/ppermute | solution.py:56
  48.7 13.1 %collective-permute-start.29 = (bf16[288,768]{1,0:T(8,128)(2,1)S(1)}, bf16[288,768]{1,0:T(8,128)(2,1)S(1)}, u32[]{:S(2)}, u32[]{:S(2)}) collective-permute-start(bf16[288,768]{1,0:T(8,128)(2,1)S(1)} %constant_dynamic-update-slice_fusion.13), channel_id=1, source_target_pairs={{0,8},{4,12},{8,0},{12,4},{16,24},{20,28},{24,16},{28,20},{1,9},{5... | collective-permute-start | bytes 1327112 | tf_op jit(solution)/shard_map/ppermute | solution.py:56
  50.2 13.2 %collective-permute-start.31 = (bf16[288,768]{1,0:T(8,128)(2,1)S(1)}, bf16[288,768]{1,0:T(8,128)(2,1)S(1)}, u32[]{:S(2)}, u32[]{:S(2)}) collective-permute-start(bf16[288,768]{1,0:T(8,128)(2,1)S(1)} %constant_dynamic-update-slice_fusion.13), channel_id=1, source_target_pairs={{0,16},{4,20},{8,24},{12,28},{16,0},{20,4},{24,8},{28,12},{1,17},{... | collective-permute-start | bytes 1327112 | tf_op jit(solution)/shard_map/ppermute | solution.py:56
  56.0 13.7 %collective-permute-start.4 = (bf16[288,768]{1,0:T(8,128)(2,1)S(1)}, bf16[288,768]{1,0:T(8,128)(2,1)S(1)}, u32[]{:S(2)}, u32[]{:S(2)}) collective-permute-start(bf16[288,768]{1,0:T(8,128)(2,1)S(1)} %constant_dynamic-update-slice_fusion.3), channel_id=1, source_target_pairs={{0,8},{4,12},{8,0},{12,4},{16,24},{20,28},{24,16},{28,20},{1,9},{5... | collective-permute-start | bytes 1327112 | tf_op jit(solution)/shard_map/ppermute | solution.py:56
  57.5 13.7 %collective-permute-start.6 = (bf16[288,768]{1,0:T(8,128)(2,1)S(1)}, bf16[288,768]{1,0:T(8,128)(2,1)S(1)}, u32[]{:S(2)}, u32[]{:S(2)}) collective-permute-start(bf16[288,768]{1,0:T(8,128)(2,1)S(1)} %constant_dynamic-update-slice_fusion.3), channel_id=1, source_target_pairs={{0,16},{4,20},{8,24},{12,28},{16,0},{20,4},{24,8},{28,12},{1,17},{... | collective-permute-start | bytes 1327112 | tf_op jit(solution)/shard_map/ppermute | solution.py:56
  61.8 11.7 %collective-permute-start.3 = (bf16[288,768]{1,0:T(8,128)(2,1)S(1)}, bf16[288,768]{1,0:T(8,128)(2,1)S(1)}, u32[]{:S(2)}, u32[]{:S(2)}) collective-permute-start(bf16[288,768]{1,0:T(8,128)(2,1)S(1)} %constant_dynamic-update-slice_fusion.3), channel_id=1, source_target_pairs={{0,4},{4,0},{8,12},{12,8},{16,20},{20,16},{24,28},{28,24},{1,5},{5... | collective-permute-start | bytes 1327112 | tf_op jit(solution)/shard_map/ppermute | solution.py:56
  69.7 13.1 %collective-permute-start.18 = (bf16[288,768]{1,0:T(8,128)(2,1)S(1)}, bf16[288,768]{1,0:T(8,128)(2,1)S(1)}, u32[]{:S(2)}, u32[]{:S(2)}) collective-permute-start(bf16[288,768]{1,0:T(8,128)(2,1)S(1)} %constant_dynamic-update-slice_fusion.8), channel_id=1, source_target_pairs={{0,8},{4,12},{8,0},{12,4},{16,24},{20,28},{24,16},{28,20},{1,9},{5... | collective-permute-start | bytes 1327112 | tf_op jit(solution)/shard_map/ppermute | solution.py:56
  71.2 13.2 %collective-permute-start.20 = (bf16[288,768]{1,0:T(8,128)(2,1)S(1)}, bf16[288,768]{1,0:T(8,128)(2,1)S(1)}, u32[]{:S(2)}, u32[]{:S(2)}) collective-permute-start(bf16[288,768]{1,0:T(8,128)(2,1)S(1)} %constant_dynamic-update-slice_fusion.8), channel_id=1, source_target_pairs={{0,16},{4,20},{8,24},{12,28},{16,0},{20,4},{24,8},{28,12},{1,17},{... | collective-permute-start | bytes 1327112 | tf_op jit(solution)/shard_map/ppermute | solution.py:56
  72.8 16.3 %collective-permute-start.33 = (bf16[144,768]{1,0:T(8,128)(2,1)S(1)}, bf16[144,768]{1,0:T(8,128)(2,1)S(1)}, u32[]{:S(2)}, u32[]{:S(2)}) collective-permute-start(bf16[144,768]{1,0:T(8,128)(2,1)S(1)} %slice.538), channel_id=1, source_target_pairs={{0,16},{4,20},{8,24},{12,28},{16,0},{20,4},{24,8},{28,12},{1,17},{... | collective-permute-start | bytes 663560 | tf_op jit(solution)/shard_map/ppermute | solution.py:56
  73.4 22.3 %collective-permute-start.34 = (bf16[144,768]{1,0:T(8,128)(2,1)S(1)}, bf16[144,768]{1,0:T(8,128)(2,1)S(1)}, u32[]{:S(2)}, u32[]{:S(2)}) collective-permute-start(bf16[144,768]{1,0:T(8,128)(2,1)S(1)} %slice.539), channel_id=1, source_target_pairs={{0,8},{4,12},{8,0},{12,4},{16,24},{20,28},{24,16},{28,20},{1,9},{5... | collective-permute-start | bytes 663560 | tf_op jit(solution)/shard_map/ppermute | solution.py:56
  74.1 19.3 %collective-permute-start.8 = (bf16[144,768]{1,0:T(8,128)(2,1)S(1)}, bf16[144,768]{1,0:T(8,128)(2,1)S(1)}, u32[]{:S(2)}, u32[]{:S(2)}) collective-permute-start(bf16[144,768]{1,0:T(8,128)(2,1)S(1)} %slice.508), channel_id=1, source_target_pairs={{0,16},{4,20},{8,24},{12,28},{16,0},{20,4},{24,8},{28,12},{1,17},{... | collective-permute-start | bytes 663560 | tf_op jit(solution)/shard_map/ppermute | solution.py:56
  82.8 13.6 %collective-permute-start.9 = (bf16[144,768]{1,0:T(8,128)(2,1)S(1)}, bf16[144,768]{1,0:T(8,128)(2,1)S(1)}, u32[]{:S(2)}, u32[]{:S(2)}) collective-permute-start(bf16[144,768]{1,0:T(8,128)(2,1)S(1)} %slice.509), channel_id=1, source_target_pairs={{0,8},{4,12},{8,0},{12,4},{16,24},{20,28},{24,16},{28,20},{1,9},{5... | collective-permute-start | bytes 663560 | tf_op jit(solution)/shard_map/ppermute | solution.py:56
  84.3 11.4 %collective-permute-start.22 = (bf16[144,768]{1,0:T(8,128)(2,1)S(1)}, bf16[144,768]{1,0:T(8,128)(2,1)S(1)}, u32[]{:S(2)}, u32[]{:S(2)}) collective-permute-start(bf16[144,768]{1,0:T(8,128)(2,1)S(1)} %slice.534), channel_id=1, source_target_pairs={{0,16},{4,20},{8,24},{12,28},{16,0},{20,4},{24,8},{28,12},{1,17},{... | collective-permute-start | bytes 663560 | tf_op jit(solution)/shard_map/ppermute | solution.py:56
  98.8 15.6 %collective-permute-start.24 = (bf16[288,768]{1,0:T(8,128)(2,1)S(1)}, bf16[288,768]{1,0:T(8,128)(2,1)S(1)}, u32[]{:S(2)}, u32[]{:S(2)}) collective-permute-start(bf16[288,768]{1,0:T(8,128)(2,1)S(1)} %constant_dynamic-update-slice_fusion.11), channel_id=1, source_target_pairs={{0,4},{4,0},{8,12},{12,8},{16,20},{20,16},{24,28},{28,24},{1,5},{5... | collective-permute-start | bytes 1327112 | tf_op jit(solution)/shard_map/ppermute | solution.py:56
  182.6 91.6 %collective-permute-start.52 = (bf16[4,4,96,768]{3,2,1,0:T(8,128)(2,1)}, bf16[4,4,96,768]{3,2,1,0:T(8,128)(2,1)}, u32[]{:S(2)}, u32[]{:S(2)}) collective-permute-start(bf16[4,4,96,768]{3,2,1,0:T(8,128)(2,1)} %pad_maximum_fusion.9), channel_id=1, source_target_pairs={{0,4},{4,0},{8,12},{12,8},{16,20},{20,16},{24,28},{28,24},{1,5},{5... | collective-permute-start | bytes 7077896 | tf_op jit(solution)/shard_map/ppermute | solution.py:56
  187.2 87.0 %collective-permute-start.44 = (bf16[4,4,96,768]{3,2,1,0:T(8,128)(2,1)}, bf16[4,4,96,768]{3,2,1,0:T(8,128)(2,1)}, u32[]{:S(2)}, u32[]{:S(2)}) collective-permute-start(bf16[4,4,96,768]{3,2,1,0:T(8,128)(2,1)} %pad_maximum_fusion.8), channel_id=1, source_target_pairs={{0,4},{4,0},{8,12},{12,8},{16,20},{20,16},{24,28},{28,24},{1,5},{5... | collective-permute-start | bytes 7077896 | tf_op jit(solution)/shard_map/ppermute | solution.py:56
  213.0 71.2 %collective-permute-start.36 = (bf16[4,4,96,768]{3,2,1,0:T(8,128)(2,1)}, bf16[4,4,96,768]{3,2,1,0:T(8,128)(2,1)}, u32[]{:S(2)}, u32[]{:S(2)}) collective-permute-start(bf16[4,4,96,768]{3,2,1,0:T(8,128)(2,1)} %pad_maximum_fusion.7), channel_id=1, source_target_pairs={{0,4},{4,0},{8,12},{12,8},{16,20},{20,16},{24,28},{28,24},{1,5},{5... | collective-permute-start | bytes 7077896 | tf_op jit(solution)/shard_map/ppermute | solution.py:56
  216.0 162.5 %collective-permute-start.68 = (f32[1152]{0:T(1024)}, f32[1152]{0:T(1024)}, u32[]{:S(2)}, u32[]{:S(2)}) collective-permute-start(f32[1152]{0:T(1024)} %concatenate.113), channel_id=1, source_target_pairs={{0,3},{1,0},{2,1},{3,2},{4,7},{5,4},{6,5},{7,6},{8,11},{9,8},{10,9... | collective-permute-start | bytes 13832 | tf_op jit(solution)/shard_map/ppermute | solution.py:53
  225.7 152.3 %collective-permute-start.70 = (f32[1152]{0:T(1024)S(1)}, f32[1152]{0:T(1024)S(1)}, u32[]{:S(2)}, u32[]{:S(2)}) collective-permute-start(f32[1152]{0:T(1024)S(1)} %concatenate.115), channel_id=1, source_target_pairs={{0,1},{1,2},{2,3},{3,0},{4,5},{5,6},{6,7},{7,4},{8,9},{9,10},{10,1... | collective-permute-start | bytes 13832 | tf_op jit(solution)/shard_map/ppermute | solution.py:53
  280.0 16.6 %collective-permute-start.53 = (bf16[2,2,96,768]{3,2,1,0:T(8,128)(2,1)S(1)}, bf16[2,2,96,768]{3,2,1,0:T(8,128)(2,1)S(1)}, u32[]{:S(2)}, u32[]{:S(2)}) collective-permute-start(bf16[2,2,96,768]{3,2,1,0:T(8,128)(2,1)S(1)} %pad_maximum_fusion.18), channel_id=1, source_target_pairs={{0,8},{4,12},{8,0},{12,4},{16,24},{20,28},{24,16},{28,20},{1,9},{5... | collective-permute-start | bytes 1769480 | tf_op jit(solution)/shard_map/ppermute | solution.py:56
  282.4 16.3 %collective-permute-start.56 = (bf16[2,2,96,768]{3,2,1,0:T(8,128)(2,1)S(1)}, bf16[2,2,96,768]{3,2,1,0:T(8,128)(2,1)S(1)}, u32[]{:S(2)}, u32[]{:S(2)}) collective-permute-start(bf16[2,2,96,768]{3,2,1,0:T(8,128)(2,1)S(1)} %pad_maximum_fusion.19), channel_id=1, source_target_pairs={{0,16},{4,20},{8,24},{12,28},{16,0},{20,4},{24,8},{28,12},{1,17},{... | collective-permute-start | bytes 1769480 | tf_op jit(solution)/shard_map/ppermute | solution.py:56
  284.2 25.0 %collective-permute-start.45 = (bf16[2,2,96,768]{3,2,1,0:T(8,128)(2,1)S(1)}, bf16[2,2,96,768]{3,2,1,0:T(8,128)(2,1)S(1)}, u32[]{:S(2)}, u32[]{:S(2)}) collective-permute-start(bf16[2,2,96,768]{3,2,1,0:T(8,128)(2,1)S(1)} %pad_maximum_fusion.16), channel_id=1, source_target_pairs={{0,8},{4,12},{8,0},{12,4},{16,24},{20,28},{24,16},{28,20},{1,9},{5... | collective-permute-start | bytes 1769480 | tf_op jit(solution)/shard_map/ppermute | solution.py:56
  296.5 14.8 %collective-permute-start.48 = (bf16[2,2,96,768]{3,2,1,0:T(8,128)(2,1)S(1)}, bf16[2,2,96,768]{3,2,1,0:T(8,128)(2,1)S(1)}, u32[]{:S(2)}, u32[]{:S(2)}) collective-permute-start(bf16[2,2,96,768]{3,2,1,0:T(8,128)(2,1)S(1)} %pad_maximum_fusion.17), channel_id=1, source_target_pairs={{0,16},{4,20},{8,24},{12,28},{16,0},{20,4},{24,8},{28,12},{1,17},{... | collective-permute-start | bytes 1769480 | tf_op jit(solution)/shard_map/ppermute | solution.py:56
  298.7 21.5 %collective-permute-start.37 = (bf16[2,2,96,768]{3,2,1,0:T(8,128)(2,1)S(1)}, bf16[2,2,96,768]{3,2,1,0:T(8,128)(2,1)S(1)}, u32[]{:S(2)}, u32[]{:S(2)}) collective-permute-start(bf16[2,2,96,768]{3,2,1,0:T(8,128)(2,1)S(1)} %pad_maximum_fusion.14), channel_id=1, source_target_pairs={{0,8},{4,12},{8,0},{12,4},{16,24},{20,28},{24,16},{28,20},{1,9},{5... | collective-permute-start | bytes 1769480 | tf_op jit(solution)/shard_map/ppermute | solution.py:56
  309.2 16.3 %collective-permute-start.40 = (bf16[2,2,96,768]{3,2,1,0:T(8,128)(2,1)S(1)}, bf16[2,2,96,768]{3,2,1,0:T(8,128)(2,1)S(1)}, u32[]{:S(2)}, u32[]{:S(2)}) collective-permute-start(bf16[2,2,96,768]{3,2,1,0:T(8,128)(2,1)S(1)} %pad_maximum_fusion.15), channel_id=1, source_target_pairs={{0,16},{4,20},{8,24},{12,28},{16,0},{20,4},{24,8},{28,12},{1,17},{... | collective-permute-start | bytes 1769480 | tf_op jit(solution)/shard_map/ppermute | solution.py:56
  311.3 20.5 %collective-permute-start.54 = (bf16[2,96,768]{2,1,0:T(8,128)(2,1)S(1)}, bf16[2,96,768]{2,1,0:T(8,128)(2,1)S(1)}, u32[]{:S(2)}, u32[]{:S(2)}) collective-permute-start(bf16[2,96,768]{2,1,0:T(8,128)(2,1)S(1)} %fusion.127), channel_id=1, source_target_pairs={{0,16},{4,20},{8,24},{12,28},{16,0},{20,4},{24,8},{28,12},{1,17},{... | collective-permute-start | bytes 884744 | tf_op jit(solution)/shard_map/ppermute | solution.py:56
  320.1 13.7 %collective-permute-start.57 = (bf16[2,96,768]{2,1,0:T(8,128)(2,1)S(1)}, bf16[2,96,768]{2,1,0:T(8,128)(2,1)S(1)}, u32[]{:S(2)}, u32[]{:S(2)}) collective-permute-start(bf16[2,96,768]{2,1,0:T(8,128)(2,1)S(1)} %fusion.126), channel_id=1, source_target_pairs={{0,8},{4,12},{8,0},{12,4},{16,24},{20,28},{24,16},{28,20},{1,9},{5... | collective-permute-start | bytes 884744 | tf_op jit(solution)/shard_map/ppermute | solution.py:56
  325.5 12.1 %collective-permute-start.46 = (bf16[2,96,768]{2,1,0:T(8,128)(2,1)S(1)}, bf16[2,96,768]{2,1,0:T(8,128)(2,1)S(1)}, u32[]{:S(2)}, u32[]{:S(2)}) collective-permute-start(bf16[2,96,768]{2,1,0:T(8,128)(2,1)S(1)} %fusion.132), channel_id=1, source_target_pairs={{0,16},{4,20},{8,24},{12,28},{16,0},{20,4},{24,8},{28,12},{1,17},{... | collective-permute-start | bytes 884744 | tf_op jit(solution)/shard_map/ppermute | solution.py:56
  340.7 16.7 %collective-permute-start.58 = (bf16[96,768]{1,0:T(8,128)(2,1)S(1)}, bf16[96,768]{1,0:T(8,128)(2,1)S(1)}, u32[]{:S(2)}, u32[]{:S(2)}) collective-permute-start(bf16[96,768]{1,0:T(8,128)(2,1)S(1)} %get-tuple-element.117), channel_id=1, source_target_pairs={{0,2},{1,3},{2,0},{3,1},{4,6},{5,7},{6,4},{7,5},{8,10},{9,11},{10,... | collective-permute-start | bytes 442376 | tf_op jit(solution)/shard_map/ppermute | solution.py:53
  344.3 13.1 %collective-permute-start.55 = (bf16[96,768]{1,0:T(8,128)(2,1)S(1)}, bf16[96,768]{1,0:T(8,128)(2,1)S(1)}, u32[]{:S(2)}, u32[]{:S(2)}) collective-permute-start(bf16[96,768]{1,0:T(8,128)(2,1)S(1)} %slice_bitcast_fusion.39), channel_id=1, source_target_pairs={{0,3},{1,0},{2,1},{3,2},{4,7},{5,4},{6,5},{7,6},{8,11},{9,8},{10,9... | collective-permute-start | bytes 442376 | tf_op jit(solution)/shard_map/ppermute | solution.py:53
  347.8 11.2 %collective-permute-start.51 = (bf16[96,768]{1,0:T(8,128)(2,1)S(1)}, bf16[96,768]{1,0:T(8,128)(2,1)S(1)}, u32[]{:S(2)}, u32[]{:S(2)}) collective-permute-start(bf16[96,768]{1,0:T(8,128)(2,1)S(1)} %get-tuple-element.116), channel_id=1, source_target_pairs={{0,1},{1,2},{2,3},{3,0},{4,5},{5,6},{6,7},{7,4},{8,9},{9,10},{10,1... | collective-permute-start | bytes 442376 | tf_op jit(solution)/shard_map/ppermute | solution.py:53
  357.4 11.1 %collective-permute-start.50 = (bf16[96,768]{1,0:T(8,128)(2,1)S(1)}, bf16[96,768]{1,0:T(8,128)(2,1)S(1)}, u32[]{:S(2)}, u32[]{:S(2)}) collective-permute-start(bf16[96,768]{1,0:T(8,128)(2,1)S(1)} %get-tuple-element.115), channel_id=1, source_target_pairs={{0,2},{1,3},{2,0},{3,1},{4,6},{5,7},{6,4},{7,5},{8,10},{9,11},{10,... | collective-permute-start | bytes 442376 | tf_op jit(solution)/shard_map/ppermute | solution.py:53
  357.4 14.5 %collective-permute-start.47 = (bf16[96,768]{1,0:T(8,128)(2,1)S(1)}, bf16[96,768]{1,0:T(8,128)(2,1)S(1)}, u32[]{:S(2)}, u32[]{:S(2)}) collective-permute-start(bf16[96,768]{1,0:T(8,128)(2,1)S(1)} %slice_bitcast_fusion.43), channel_id=1, source_target_pairs={{0,3},{1,0},{2,1},{3,2},{4,7},{5,4},{6,5},{7,6},{8,11},{9,8},{10,9... | collective-permute-start | bytes 442376 | tf_op jit(solution)/shard_map/ppermute | solution.py:53
  358.9 13.4 %collective-permute-start.43 = (bf16[96,768]{1,0:T(8,128)(2,1)S(1)}, bf16[96,768]{1,0:T(8,128)(2,1)S(1)}, u32[]{:S(2)}, u32[]{:S(2)}) collective-permute-start(bf16[96,768]{1,0:T(8,128)(2,1)S(1)} %get-tuple-element.114), channel_id=1, source_target_pairs={{0,1},{1,2},{2,3},{3,0},{4,5},{5,6},{6,7},{7,4},{8,9},{9,10},{10,1... | collective-permute-start | bytes 442376 | tf_op jit(solution)/shard_map/ppermute | solution.py:53
  377.8 22.6 %collective-permute-start.60 = (bf16[288,768]{1,0:T(8,128)(2,1)S(1)}, bf16[288,768]{1,0:T(8,128)(2,1)S(1)}, u32[]{:S(2)}, u32[]{:S(2)}) collective-permute-start(bf16[288,768]{1,0:T(8,128)(2,1)S(1)} %pad_maximum_fusion.20), channel_id=1, source_target_pairs={{0,4},{4,0},{8,12},{12,8},{16,20},{20,16},{24,28},{28,24},{1,5},{5... | collective-permute-start | bytes 1327112 | tf_op jit(solution)/shard_map/ppermute | solution.py:56
  377.9 21.5 %collective-permute-start.61 = (bf16[288,768]{1,0:T(8,128)(2,1)S(1)}, bf16[288,768]{1,0:T(8,128)(2,1)S(1)}, u32[]{:S(2)}, u32[]{:S(2)}) collective-permute-start(bf16[288,768]{1,0:T(8,128)(2,1)S(1)} %pad_maximum_fusion.20), channel_id=1, source_target_pairs={{0,8},{4,12},{8,0},{12,4},{16,24},{20,28},{24,16},{28,20},{1,9},{5... | collective-permute-start | bytes 1327112 | tf_op jit(solution)/shard_map/ppermute | solution.py:56
  378.0 21.7 %collective-permute-start.63 = (bf16[288,768]{1,0:T(8,128)(2,1)S(1)}, bf16[288,768]{1,0:T(8,128)(2,1)S(1)}, u32[]{:S(2)}, u32[]{:S(2)}) collective-permute-start(bf16[288,768]{1,0:T(8,128)(2,1)S(1)} %pad_maximum_fusion.20), channel_id=1, source_target_pairs={{0,16},{4,20},{8,24},{12,28},{16,0},{20,4},{24,8},{28,12},{1,17},{... | collective-permute-start | bytes 1327112 | tf_op jit(solution)/shard_map/ppermute | solution.py:56
  (100 other events, 707.1 us)
where the time goes:
time: 423 us; the launch traced here: 418 us
  waiting for transfers between devices  111 us (26%)
  starting transfers between devices  79.4 us (19%)
  matrix products  74.4 us (18%)
  blocking collectives  59.8 us (14%)
  local copies, waits for them, and re-layouts  53.9 us (13%)
  other arithmetic  36.1 us (9%)
    ppermute x47, waiting for transfers between devices, flip(): return lax.ppermute(x, 'dp', [(i, i ^ bit) for i in range(self.dp)])  77.7 us
    dot_general x48, matrix products, dot(): lax.dot_general(left, right, ((dims[:1], dims[1:]), ((), ())), preferred_...  48.4 us
    ppermute x24, starting transfers between devices, shift(): lax.ppermute(x, 'mp', [(i, (i + by) % self.mp) for i in range(self.mp)])  41.3 us
    psum x1, blocking collectives, per_device(): shared = lax.psum(shared, ('dp', 'mp'))  40.8 us
    ppermute x47, starting transfers between devices, flip(): return lax.ppermute(x, 'dp', [(i, i ^ bit) for i in range(self.dp)])  38.1 us
    ppermute x24, waiting for transfers between devices, shift(): lax.ppermute(x, 'mp', [(i, (i + by) % self.mp) for i in range(self.mp)])  32.9 us
    unnamed x229, local copies, waits for them, and re-layouts  27.9 us
    psum x1, blocking collectives, per_device(): mine = lax.psum(mine, 'dp')  18.9 us
  transfers between devices with their start and end apart: 71, of which 36 were waited for; matrix products, arithmetic and copies ran while one was open for 19% of the time, Pallas kernels for 0%

commit v1 on v0

--- a/solution.py
+++ b/solution.py
@@ -234,7 +234,8 @@
     whole = whole.transpose(1, 0, 2, 3).reshape(3, width, width).astype(f32)
     g_a, g_u, g_d = (whole[0], whole[1], whole[2])
     shared = jnp.stack([g_gain1, g_bias1, g_b_out, g_gain2, g_bias2, g_b_down])
-    shared = lax.psum(shared, ("dp", "mp"))
+    forms_choose = lambda vals: lax.psum(lax.psum(vals, axis_name="mp"), axis_name="dp")
+    shared = forms_choose(shared)
     split = [jnp.concatenate([g_bq[s], g_bv[s], g_b_up[s]]) for s in slots]
     mine = split[0] + sum((links.shift(split[s], -s) for s in range(1, mp)))
     mine = lax.psum(mine, "dp")

time: 423 us -> 398 us (0.941)
  blocking collectives: 59.8 us -> 40.7 us
  matrix products: 74.4 us -> 67.4 us
    psum x1, blocking collectives: 40.8 us -> 16.5 us  [per_device(): lax.psum(vals, axis_name='mp')]
    ppermute x47, waiting for transfers between devices: 77.7 us -> 89.4 us  [flip(): return lax.ppermute(x, 'dp', [(i, i ^ bit) for i in range(self.dp)])]
    ppermute x24, waiting for transfers between devices: 32.9 us -> 24 us  [shift(): lax.ppermute(x, 'mp', [(i, (i + by) % self.mp) for i in range(self.mp)])]
    ppermute x24, starting transfers between devices: 41.3 us -> 48.2 us  [shift(): lax.ppermute(x, 'mp', [(i, (i + by) % self.mp) for i in range(self.mp)])]
    psum x1, blocking collectives: 18.9 us -> 24.1 us  [per_device(): mine = lax.psum(mine, 'dp')]
    ppermute x47, starting transfers between devices: 38.1 us -> 33.4 us  [flip(): return lax.ppermute(x, 'dp', [(i, i ^ bit) for i in range(self.dp)])]
    unnamed x229 -> x207, local copies, waits for them, and re-layouts: 27.9 us -> 29.1 us
  transfers between devices with their start and end apart: 71 -> 71, of which waited for: 36 -> 33; matrix products, arithmetic and copies ran while one was open for 19% -> 19% of each run, Pallas kernels for 0% -> 0%
where the time goes in v1:
time: 398 us; the launch traced here: 393 us
  waiting for transfers between devices  113 us (28%)
  starting transfers between devices  81.6 us (21%)
  matrix products  67.4 us (17%)
  local copies, waits for them, and re-layouts  52.5 us (13%)
  blocking collectives  40.7 us (10%)
  other arithmetic  34.3 us (9%)
    ppermute x47, waiting for transfers between devices, flip(): return lax.ppermute(x, 'dp', [(i, i ^ bit) for i in range(self.dp)])  89.4 us
    ppermute x24, starting transfers between devices, shift(): lax.ppermute(x, 'mp', [(i, (i + by) % self.mp) for i in range(self.mp)])  48.2 us
    dot_general x48, matrix products, dot(): lax.dot_general(left, right, ((dims[:1], dims[1:]), ((), ())), preferred_...  46.1 us
    ppermute x47, starting transfers between devices, flip(): return lax.ppermute(x, 'dp', [(i, i ^ bit) for i in range(self.dp)])  33.4 us
    unnamed x207, local copies, waits for them, and re-layouts  29.1 us
    psum x1, blocking collectives, per_device(): mine = lax.psum(mine, 'dp')  24.1 us
    ppermute x24, waiting for transfers between devices, shift(): lax.ppermute(x, 'mp', [(i, (i + by) % self.mp) for i in range(self.mp)])  24 us
    psum x1, blocking collectives, per_device(): lax.psum(vals, axis_name='mp')  16.5 us
  transfers between devices with their start and end apart: 71, of which 33 were waited for; matrix products, arithmetic and copies ran while one was open for 19% of the time, Pallas kernels for 0%

profile of v1, /device:TPU:0, one launch (start us, length us, event | category | flops | bytes accessed | tf_op | source)
XLA Modules:
  0.0 393.1 jit_solution(18210828468788632115)
XLA Ops:
  2.4 3.0 collective-permute-start.25
  5.5 2.6 collective-permute-start.26
  9.4 2.1 concatenate.93
  17.5 2.0 copy.72
  31.5 3.6 collective-permute-done.11
  39.1 3.0 collective-permute-start.15
  44.5 3.0 collective-permute-done.14
  51.8 4.2 %collective-permute-done.15 = bf16[96,768]{1,0:T(8,128)(2,1)S(1)} collective-permute-done((bf16[96,768]{1,0:T(8,128)(2,1)S(1)}, bf16[96,768]{1,0:T(8,128)(2,1)S(1)}, u32[]{:S(2)}, u32[]{:S(2)}) %collective-permute-start.15) | collective-permute-done | bytes 147488 | tf_op jit(solution)/shard_map/ppermute | solution.py:53
  59.1 2.6 collective-permute-done.29
  63.3 6.3 %collective-permute-done.4 = bf16[288,768]{1,0:T(8,128)(2,1)S(1)} collective-permute-done((bf16[288,768]{1,0:T(8,128)(2,1)S(1)}, bf16[288,768]{1,0:T(8,128)(2,1)S(1)}, u32[]{:S(2)}, u32[]{:S(2)}) %collective-permute-start.4) | collective-permute-done | bytes 442400 | tf_op jit(solution)/shard_map/ppermute | solution.py:56
  75.7 7.0 %collective-permute-done.18 = bf16[288,768]{1,0:T(8,128)(2,1)S(1)} collective-permute-done((bf16[288,768]{1,0:T(8,128)(2,1)S(1)}, bf16[288,768]{1,0:T(8,128)(2,1)S(1)}, u32[]{:S(2)}, u32[]{:S(2)}) %collective-permute-start.18) | collective-permute-done | bytes 442400 | tf_op jit(solution)/shard_map/ppermute | solution.py:56
  85.9 3.2 collective-permute-done.33
  89.6 3.8 collective-permute-done.8
  93.4 2.3 collective-permute-done.22
  116.2 2.0 multiply_convert_fusion.7
  119.0 1.9 multiply_convert_fusion.5
  171.5 2.0 copy-done.6
  176.2 2.0 copy-done.7
  186.5 2.4 copy.90
  191.7 2.4 copy.89
  197.0 2.4 copy.88
  199.6 9.2 %collective-permute-start.70 = (f32[1152]{0:T(1024)S(1)}, f32[1152]{0:T(1024)S(1)}, u32[]{:S(2)}, u32[]{:S(2)}) collective-permute-start(f32[1152]{0:T(1024)S(1)} %concatenate.115), channel_id=1, source_target_pairs={{0,1},{1,2},{2,3},{3,0},{4,5},{5,6},{6,7},{7,4},{8,9},{9,10},{10,1... | collective-permute-start | bytes 13832 | tf_op jit(solution)/shard_map/ppermute | solution.py:53
  209.3 3.9 %collective-permute-start.69 = (f32[1152]{0:T(1024)S(1)}, f32[1152]{0:T(1024)S(1)}, u32[]{:S(2)}, u32[]{:S(2)}) collective-permute-start(f32[1152]{0:T(1024)S(1)} %concatenate.114), channel_id=1, source_target_pairs={{0,2},{1,3},{2,0},{3,1},{4,6},{5,7},{6,4},{7,5},{8,10},{9,11},{10,... | collective-permute-start | bytes 13832 | tf_op jit(solution)/shard_map/ppermute | solution.py:53
  213.4 2.3 pad_maximum_fusion
  215.9 2.0 copy-done.5
  224.2 1.9 add_convert_fusion
  226.1 16.5 %psum.22 = f32[6,768]{1,0:T(8,128)S(1)} all-reduce(f32[6,768]{1,0:T(8,128)S(1)} %stack.372), channel_id=1, replica_groups=mesh['dp'=8,'mp'=4] {'mp'}, use_global_device_ids=true, to_apply=%region_39.40 | all-reduce | flops 4608 | bytes 36864 | tf_op jit(solution)/shard_map/psum | solution.py:237
  242.9 24.1 %all-reduce = (f32[1152]{0:T(1024)S(1)}, f32[6,768]{1,0:T(8,128)S(1)}) all-reduce(f32[1152]{0:T(1024)S(1)} %add_add_fusion.3, f32[6,768]{1,0:T(8,128)S(1)} %psum.22), channel_id=1, replica_groups=mesh['dp'=8,'mp'=4] {'dp'}, use_global_device_ids=true, to_apply=%region_32.33 | all-reduce | flops 5760 | bytes 46080 | tf_op jit(solution)/shard_map/psum | solution.py:241
  267.7 5.6 %fusion.59 = (bf16[4,96,768]{2,1,0:T(8,128)(2,1)S(1)}, bf16[4,96,768]{2,1,0:T(8,128)(2,1)S(1)}, bf16[4,96,768]{2,1,0:T(8,128)(2,1)S(1)}, bf16[4,96,768]{2,1,0:T(...) fusion(bf16[4,8,96,768]{3,2,0,1:T(8,128)(2,1)} %copy-done.6, ...), kind=kLoop, calls=%fused_computation.155 | loop fusion | flops 9437184 | bytes 14155792 | tf_op jit(solution)/shard_map/convert_element_type | solution.py:96
  274.3 2.1 collective-permute-start.45
  278.1 2.2 fusion.67
  280.7 9.1 %collective-permute-done.53 = bf16[2,2,96,768]{3,2,1,0:T(8,128)(2,1)S(1)} collective-permute-done((bf16[2,2,96,768]{3,2,1,0:T(8,128)(2,1)S(1)}, bf16[2,2,96,768]{3,2,1,0:T(8,128)(2,1)S(1)}, u32[]{:S(2)}, u32[]{:S(2)}) %collective-permute-start.53) | collective-permute-done | bytes 589856 | tf_op jit(solution)/shard_map/ppermute | solution.py:56
  292.0 10.4 %collective-permute-done.45 = bf16[2,2,96,768]{3,2,1,0:T(8,128)(2,1)S(1)} collective-permute-done((bf16[2,2,96,768]{3,2,1,0:T(8,128)(2,1)S(1)}, bf16[2,2,96,768]{3,2,1,0:T(8,128)(2,1)S(1)}, u32[]{:S(2)}, u32[]{:S(2)}) %collective-permute-start.45) | collective-permute-done | bytes 589856 | tf_op jit(solution)/shard_map/ppermute | solution.py:56
  303.2 11.9 %collective-permute-done.37 = bf16[2,2,96,768]{3,2,1,0:T(8,128)(2,1)S(1)} collective-permute-done((bf16[2,2,96,768]{3,2,1,0:T(8,128)(2,1)S(1)}, bf16[2,2,96,768]{3,2,1,0:T(8,128)(2,1)S(1)}, u32[]{:S(2)}, u32[]{:S(2)}) %collective-permute-start.37) | collective-permute-done | bytes 589856 | tf_op jit(solution)/shard_map/ppermute | solution.py:56
  315.8 5.8 %collective-permute-done.54 = bf16[2,96,768]{2,1,0:T(8,128)(2,1)S(1)} collective-permute-done((bf16[2,96,768]{2,1,0:T(8,128)(2,1)S(1)}, bf16[2,96,768]{2,1,0:T(8,128)(2,1)S(1)}, u32[]{:S(2)}, u32[]{:S(2)}) %collective-permute-start.54) | collective-permute-done | bytes 294944 | tf_op jit(solution)/shard_map/ppermute | solution.py:56
  321.6 2.0 collective-permute-start.41
  323.9 4.0 %collective-permute-done.46 = bf16[2,96,768]{2,1,0:T(8,128)(2,1)S(1)} collective-permute-done((bf16[2,96,768]{2,1,0:T(8,128)(2,1)S(1)}, bf16[2,96,768]{2,1,0:T(8,128)(2,1)S(1)}, u32[]{:S(2)}, u32[]{:S(2)}) %collective-permute-start.46) | collective-permute-done | bytes 294944 | tf_op jit(solution)/shard_map/ppermute | solution.py:56
  329.8 2.0 collective-permute-done.38
  333.7 2.2 collective-permute-start.47
  335.9 5.2 %collective-permute-done.58 = bf16[96,768]{1,0:T(8,128)(2,1)S(1)} collective-permute-done((bf16[96,768]{1,0:T(8,128)(2,1)S(1)}, bf16[96,768]{1,0:T(8,128)(2,1)S(1)}, u32[]{:S(2)}, u32[]{:S(2)}) %collective-permute-start.58) | collective-permute-done | bytes 147488 | tf_op jit(solution)/shard_map/ppermute | solution.py:53
  341.8 7.9 %collective-permute-start.42 = (bf16[96,768]{1,0:T(8,128)(2,1)S(1)}, bf16[96,768]{1,0:T(8,128)(2,1)S(1)}, u32[]{:S(2)}, u32[]{:S(2)}) collective-permute-start(bf16[96,768]{1,0:T(8,128)(2,1)S(1)} %get-tuple-element.115), channel_id=1, source_target_pairs={{0,2},{1,3},{2,0},{3,1},{4,6},{5,7},{6,4},{7,5},{8,10},{9,11},{10,... | collective-permute-start | bytes 442376 | tf_op jit(solution)/shard_map/ppermute | solution.py:53
  349.7 3.6 collective-permute-start.39
  353.5 6.8 %collective-permute-done.42 = bf16[96,768]{1,0:T(8,128)(2,1)S(1)} collective-permute-done((bf16[96,768]{1,0:T(8,128)(2,1)S(1)}, bf16[96,768]{1,0:T(8,128)(2,1)S(1)}, u32[]{:S(2)}, u32[]{:S(2)}) %collective-permute-start.42) | collective-permute-done | bytes 147488 | tf_op jit(solution)/shard_map/ppermute | solution.py:53
  360.9 2.1 collective-permute-start.63
  364.3 8.7 %collective-permute-done.61 = bf16[288,768]{1,0:T(8,128)(2,1)S(1)} collective-permute-done((bf16[288,768]{1,0:T(8,128)(2,1)S(1)}, bf16[288,768]{1,0:T(8,128)(2,1)S(1)}, u32[]{:S(2)}, u32[]{:S(2)}) %collective-permute-start.61) | collective-permute-done | bytes 442400 | tf_op jit(solution)/shard_map/ppermute | solution.py:56
  373.1 2.5 collective-permute-start.65
  376.5 4.3 %collective-permute-done.65 = bf16[144,768]{1,0:T(8,128)(2,1)S(1)} collective-permute-done((bf16[144,768]{1,0:T(8,128)(2,1)S(1)}, bf16[144,768]{1,0:T(8,128)(2,1)S(1)}, u32[]{:S(2)}, u32[]{:S(2)}) %collective-permute-start.65) | collective-permute-done | bytes 221216 | tf_op jit(solution)/shard_map/ppermute | solution.py:56
  385.4 2.7 fusion.180
  (539 shorter events, 165.3 us)
Async XLA Ops:
  2.4 32.7 %collective-permute-start.25 = (bf16[96,768]{1,0:T(8,128)(2,1)}, bf16[96,768]{1,0:T(8,128)(2,1)}, u32[]{:S(2)}, u32[]{:S(2)}) collective-permute-start(bf16[96,768]{1,0:T(8,128)(2,1)} %constant_dynamic-slice_fusion), channel_id=1, source_target_pairs={{0,1},{1,2},{2,3},{3,0},{4,5},{5,6},{6,7},{7,4},{8,9},{9,10},{10,1... | collective-permute-start | bytes 442376 | tf_op jit(solution)/shard_map/ppermute | solution.py:53
  5.5 31.1 %collective-permute-start.26 = (bf16[96,768]{1,0:T(8,128)(2,1)}, bf16[96,768]{1,0:T(8,128)(2,1)}, u32[]{:S(2)}, u32[]{:S(2)}) collective-permute-start(bf16[96,768]{1,0:T(8,128)(2,1)} %constant_dynamic-slice_fusion), channel_id=1, source_target_pairs={{0,2},{1,3},{2,0},{3,1},{4,6},{5,7},{6,4},{7,5},{8,10},{9,11},{10,... | collective-permute-start | bytes 442376 | tf_op jit(solution)/shard_map/ppermute | solution.py:53
  8.1 31.1 %collective-permute-start.27 = (bf16[96,768]{1,0:T(8,128)(2,1)}, bf16[96,768]{1,0:T(8,128)(2,1)}, u32[]{:S(2)}, u32[]{:S(2)}) collective-permute-start(bf16[96,768]{1,0:T(8,128)(2,1)} %constant_dynamic-slice_fusion), channel_id=1, source_target_pairs={{0,3},{1,0},{2,1},{3,2},{4,7},{5,4},{6,5},{7,6},{8,11},{9,8},{10,9... | collective-permute-start | bytes 442376 | tf_op jit(solution)/shard_map/ppermute | solution.py:53
  11.5 18.0 %collective-permute-start.13 = (bf16[1152]{0:T(1024)(128)(2,1)S(1)}, bf16[1152]{0:T(1024)(128)(2,1)S(1)}, u32[]{:S(2)}, u32[]{:S(2)}) collective-permute-start(bf16[1152]{0:T(1024)(128)(2,1)S(1)} %concatenate.93), channel_id=1, source_target_pairs={{0,3},{1,0},{2,1},{3,2},{4,7},{5,4},{6,5},{7,6},{8,11},{9,8},{10,9... | collective-permute-start | bytes 6920 | tf_op jit(solution)/shard_map/ppermute | solution.py:53
  11.9 17.7 %collective-permute-start.12 = (bf16[1152]{0:T(1024)(128)(2,1)S(1)}, bf16[1152]{0:T(1024)(128)(2,1)S(1)}, u32[]{:S(2)}, u32[]{:S(2)}) collective-permute-start(bf16[1152]{0:T(1024)(128)(2,1)S(1)} %concatenate.93), channel_id=1, source_target_pairs={{0,2},{1,3},{2,0},{3,1},{4,6},{5,7},{6,4},{7,5},{8,10},{9,11},{10,... | collective-permute-start | bytes 6920 | tf_op jit(solution)/shard_map/ppermute | solution.py:53
  29.7 13.4 %collective-permute-start = (bf16[96,768]{1,0:T(8,128)(2,1)S(1)}, bf16[96,768]{1,0:T(8,128)(2,1)S(1)}, u32[]{:S(2)}, u32[]{:S(2)}) collective-permute-start(bf16[96,768]{1,0:T(8,128)(2,1)S(1)} %fusion.167), channel_id=1, source_target_pairs={{0,1},{1,2},{2,3},{3,0},{4,5},{5,6},{6,7},{7,4},{8,9},{9,10},{10,1... | collective-permute-start | bytes 442376 | tf_op jit(solution)/shard_map/ppermute | solution.py:53
  35.1 13.5 %collective-permute-start.1 = (bf16[96,768]{1,0:T(8,128)(2,1)S(1)}, bf16[96,768]{1,0:T(8,128)(2,1)S(1)}, u32[]{:S(2)}, u32[]{:S(2)}) collective-permute-start(bf16[96,768]{1,0:T(8,128)(2,1)S(1)} %fusion.167), channel_id=1, source_target_pairs={{0,2},{1,3},{2,0},{3,1},{4,6},{5,7},{6,4},{7,5},{8,10},{9,11},{10,... | collective-permute-start | bytes 442376 | tf_op jit(solution)/shard_map/ppermute | solution.py:53
  35.2 15.0 %collective-permute-start.2 = (bf16[96,768]{1,0:T(8,128)(2,1)S(1)}, bf16[96,768]{1,0:T(8,128)(2,1)S(1)}, u32[]{:S(2)}, u32[]{:S(2)}) collective-permute-start(bf16[96,768]{1,0:T(8,128)(2,1)S(1)} %fusion.167), channel_id=1, source_target_pairs={{0,3},{1,0},{2,1},{3,2},{4,7},{5,4},{6,5},{7,6},{8,11},{9,8},{10,9... | collective-permute-start | bytes 442376 | tf_op jit(solution)/shard_map/ppermute | solution.py:53
  39.1 16.8 %collective-permute-start.15 = (bf16[96,768]{1,0:T(8,128)(2,1)S(1)}, bf16[96,768]{1,0:T(8,128)(2,1)S(1)}, u32[]{:S(2)}, u32[]{:S(2)}) collective-permute-start(bf16[96,768]{1,0:T(8,128)(2,1)S(1)} %constant_dynamic-slice_fusion.1), channel_id=1, source_target_pairs={{0,2},{1,3},{2,0},{3,1},{4,6},{5,7},{6,4},{7,5},{8,10},{9,11},{10,... | collective-permute-start | bytes 442376 | tf_op jit(solution)/shard_map/ppermute | solution.py:53
  43.1 14.4 %collective-permute-start.16 = (bf16[96,768]{1,0:T(8,128)(2,1)S(1)}, bf16[96,768]{1,0:T(8,128)(2,1)S(1)}, u32[]{:S(2)}, u32[]{:S(2)}) collective-permute-start(bf16[96,768]{1,0:T(8,128)(2,1)S(1)} %constant_dynamic-slice_fusion.1), channel_id=1, source_target_pairs={{0,3},{1,0},{2,1},{3,2},{4,7},{5,4},{6,5},{7,6},{8,11},{9,8},{10,9... | collective-permute-start | bytes 442376 | tf_op jit(solution)/shard_map/ppermute | solution.py:53
  47.5 25.3 %collective-permute-start.28 = (bf16[288,768]{1,0:T(8,128)(2,1)S(1)}, bf16[288,768]{1,0:T(8,128)(2,1)S(1)}, u32[]{:S(2)}, u32[]{:S(2)}) collective-permute-start(bf16[288,768]{1,0:T(8,128)(2,1)S(1)} %constant_dynamic-update-slice_fusion.13), channel_id=1, source_target_pairs={{0,4},{4,0},{8,12},{12,8},{16,20},{20,16},{24,28},{28,24},{1,5},{5... | collective-permute-start | bytes 1327112 | tf_op jit(solution)/shard_map/ppermute | solution.py:56
  48.6 13.1 %collective-permute-start.29 = (bf16[288,768]{1,0:T(8,128)(2,1)S(1)}, bf16[288,768]{1,0:T(8,128)(2,1)S(1)}, u32[]{:S(2)}, u32[]{:S(2)}) collective-permute-start(bf16[288,768]{1,0:T(8,128)(2,1)S(1)} %constant_dynamic-update-slice_fusion.13), channel_id=1, source_target_pairs={{0,8},{4,12},{8,0},{12,4},{16,24},{20,28},{24,16},{28,20},{1,9},{5... | collective-permute-start | bytes 1327112 | tf_op jit(solution)/shard_map/ppermute | solution.py:56
  50.1 13.2 %collective-permute-start.31 = (bf16[288,768]{1,0:T(8,128)(2,1)S(1)}, bf16[288,768]{1,0:T(8,128)(2,1)S(1)}, u32[]{:S(2)}, u32[]{:S(2)}) collective-permute-start(bf16[288,768]{1,0:T(8,128)(2,1)S(1)} %constant_dynamic-update-slice_fusion.13), channel_id=1, source_target_pairs={{0,16},{4,20},{8,24},{12,28},{16,0},{20,4},{24,8},{28,12},{1,17},{... | collective-permute-start | bytes 1327112 | tf_op jit(solution)/shard_map/ppermute | solution.py:56
  56.0 13.7 %collective-permute-start.4 = (bf16[288,768]{1,0:T(8,128)(2,1)S(1)}, bf16[288,768]{1,0:T(8,128)(2,1)S(1)}, u32[]{:S(2)}, u32[]{:S(2)}) collective-permute-start(bf16[288,768]{1,0:T(8,128)(2,1)S(1)} %constant_dynamic-update-slice_fusion.3), channel_id=1, source_target_pairs={{0,8},{4,12},{8,0},{12,4},{16,24},{20,28},{24,16},{28,20},{1,9},{5... | collective-permute-start | bytes 1327112 | tf_op jit(solution)/shard_map/ppermute | solution.py:56
  57.5 13.7 %collective-permute-start.6 = (bf16[288,768]{1,0:T(8,128)(2,1)S(1)}, bf16[288,768]{1,0:T(8,128)(2,1)S(1)}, u32[]{:S(2)}, u32[]{:S(2)}) collective-permute-start(bf16[288,768]{1,0:T(8,128)(2,1)S(1)} %constant_dynamic-update-slice_fusion.3), channel_id=1, source_target_pairs={{0,16},{4,20},{8,24},{12,28},{16,0},{20,4},{24,8},{28,12},{1,17},{... | collective-permute-start | bytes 1327112 | tf_op jit(solution)/shard_map/ppermute | solution.py:56
  69.6 13.1 %collective-permute-start.18 = (bf16[288,768]{1,0:T(8,128)(2,1)S(1)}, bf16[288,768]{1,0:T(8,128)(2,1)S(1)}, u32[]{:S(2)}, u32[]{:S(2)}) collective-permute-start(bf16[288,768]{1,0:T(8,128)(2,1)S(1)} %constant_dynamic-update-slice_fusion.8), channel_id=1, source_target_pairs={{0,8},{4,12},{8,0},{12,4},{16,24},{20,28},{24,16},{28,20},{1,9},{5... | collective-permute-start | bytes 1327112 | tf_op jit(solution)/shard_map/ppermute | solution.py:56
  71.1 13.2 %collective-permute-start.20 = (bf16[288,768]{1,0:T(8,128)(2,1)S(1)}, bf16[288,768]{1,0:T(8,128)(2,1)S(1)}, u32[]{:S(2)}, u32[]{:S(2)}) collective-permute-start(bf16[288,768]{1,0:T(8,128)(2,1)S(1)} %constant_dynamic-update-slice_fusion.8), channel_id=1, source_target_pairs={{0,16},{4,20},{8,24},{12,28},{16,0},{20,4},{24,8},{28,12},{1,17},{... | collective-permute-start | bytes 1327112 | tf_op jit(solution)/shard_map/ppermute | solution.py:56
  72.8 16.3 %collective-permute-start.33 = (bf16[144,768]{1,0:T(8,128)(2,1)S(1)}, bf16[144,768]{1,0:T(8,128)(2,1)S(1)}, u32[]{:S(2)}, u32[]{:S(2)}) collective-permute-start(bf16[144,768]{1,0:T(8,128)(2,1)S(1)} %slice.538), channel_id=1, source_target_pairs={{0,16},{4,20},{8,24},{12,28},{16,0},{20,4},{24,8},{28,12},{1,17},{... | collective-permute-start | bytes 663560 | tf_op jit(solution)/shard_map/ppermute | solution.py:56
  73.4 22.4 %collective-permute-start.34 = (bf16[144,768]{1,0:T(8,128)(2,1)S(1)}, bf16[144,768]{1,0:T(8,128)(2,1)S(1)}, u32[]{:S(2)}, u32[]{:S(2)}) collective-permute-start(bf16[144,768]{1,0:T(8,128)(2,1)S(1)} %slice.539), channel_id=1, source_target_pairs={{0,8},{4,12},{8,0},{12,4},{16,24},{20,28},{24,16},{28,20},{1,9},{5... | collective-permute-start | bytes 663560 | tf_op jit(solution)/shard_map/ppermute | solution.py:56
  74.1 19.3 %collective-permute-start.8 = (bf16[144,768]{1,0:T(8,128)(2,1)S(1)}, bf16[144,768]{1,0:T(8,128)(2,1)S(1)}, u32[]{:S(2)}, u32[]{:S(2)}) collective-permute-start(bf16[144,768]{1,0:T(8,128)(2,1)S(1)} %slice.508), channel_id=1, source_target_pairs={{0,16},{4,20},{8,24},{12,28},{16,0},{20,4},{24,8},{28,12},{1,17},{... | collective-permute-start | bytes 663560 | tf_op jit(solution)/shard_map/ppermute | solution.py:56
  82.7 13.6 %collective-permute-start.9 = (bf16[144,768]{1,0:T(8,128)(2,1)S(1)}, bf16[144,768]{1,0:T(8,128)(2,1)S(1)}, u32[]{:S(2)}, u32[]{:S(2)}) collective-permute-start(bf16[144,768]{1,0:T(8,128)(2,1)S(1)} %slice.509), channel_id=1, source_target_pairs={{0,8},{4,12},{8,0},{12,4},{16,24},{20,28},{24,16},{28,20},{1,9},{5... | collective-permute-start | bytes 663560 | tf_op jit(solution)/shard_map/ppermute | solution.py:56
  98.8 15.6 %collective-permute-start.24 = (bf16[288,768]{1,0:T(8,128)(2,1)S(1)}, bf16[288,768]{1,0:T(8,128)(2,1)S(1)}, u32[]{:S(2)}, u32[]{:S(2)}) collective-permute-start(bf16[288,768]{1,0:T(8,128)(2,1)S(1)} %constant_dynamic-update-slice_fusion.11), channel_id=1, source_target_pairs={{0,4},{4,0},{8,12},{12,8},{16,20},{20,16},{24,28},{28,24},{1,5},{5... | collective-permute-start | bytes 1327112 | tf_op jit(solution)/shard_map/ppermute | solution.py:56
  175.2 92.4 %collective-permute-start.52 = (bf16[4,4,96,768]{3,2,1,0:T(8,128)(2,1)}, bf16[4,4,96,768]{3,2,1,0:T(8,128)(2,1)}, u32[]{:S(2)}, u32[]{:S(2)}) collective-permute-start(bf16[4,4,96,768]{3,2,1,0:T(8,128)(2,1)} %pad_maximum_fusion.9), channel_id=1, source_target_pairs={{0,4},{4,0},{8,12},{12,8},{16,20},{20,16},{24,28},{28,24},{1,5},{5... | collective-permute-start | bytes 7077896 | tf_op jit(solution)/shard_map/ppermute | solution.py:56
  179.9 87.8 %collective-permute-start.44 = (bf16[4,4,96,768]{3,2,1,0:T(8,128)(2,1)}, bf16[4,4,96,768]{3,2,1,0:T(8,128)(2,1)}, u32[]{:S(2)}, u32[]{:S(2)}) collective-permute-start(bf16[4,4,96,768]{3,2,1,0:T(8,128)(2,1)} %pad_maximum_fusion.8), channel_id=1, source_target_pairs={{0,4},{4,0},{8,12},{12,8},{16,20},{20,16},{24,28},{28,24},{1,5},{5... | collective-permute-start | bytes 7077896 | tf_op jit(solution)/shard_map/ppermute | solution.py:56
  199.6 43.3 %collective-permute-start.70 = (f32[1152]{0:T(1024)S(1)}, f32[1152]{0:T(1024)S(1)}, u32[]{:S(2)}, u32[]{:S(2)}) collective-permute-start(f32[1152]{0:T(1024)S(1)} %concatenate.115), channel_id=1, source_target_pairs={{0,1},{1,2},{2,3},{3,0},{4,5},{5,6},{6,7},{7,4},{8,9},{9,10},{10,1... | collective-permute-start | bytes 13832 | tf_op jit(solution)/shard_map/ppermute | solution.py:53
  209.1 33.8 %collective-permute-start.68 = (f32[1152]{0:T(1024)S(1)}, f32[1152]{0:T(1024)S(1)}, u32[]{:S(2)}, u32[]{:S(2)}) collective-permute-start(f32[1152]{0:T(1024)S(1)} %concatenate.113), channel_id=1, source_target_pairs={{0,3},{1,0},{2,1},{3,2},{4,7},{5,4},{6,5},{7,6},{8,11},{9,8},{10,9... | collective-permute-start | bytes 13832 | tf_op jit(solution)/shard_map/ppermute | solution.py:53
  209.3 33.6 %collective-permute-start.69 = (f32[1152]{0:T(1024)S(1)}, f32[1152]{0:T(1024)S(1)}, u32[]{:S(2)}, u32[]{:S(2)}) collective-permute-start(f32[1152]{0:T(1024)S(1)} %concatenate.114), channel_id=1, source_target_pairs={{0,2},{1,3},{2,0},{3,1},{4,6},{5,7},{6,4},{7,5},{8,10},{9,11},{10,... | collective-permute-start | bytes 13832 | tf_op jit(solution)/shard_map/ppermute | solution.py:53
  242.9 35.2 %collective-permute-start.36 = (bf16[4,4,96,768]{3,2,1,0:T(8,128)(2,1)}, bf16[4,4,96,768]{3,2,1,0:T(8,128)(2,1)}, u32[]{:S(2)}, u32[]{:S(2)}) collective-permute-start(bf16[4,4,96,768]{3,2,1,0:T(8,128)(2,1)} %pad_maximum_fusion.7), channel_id=1, source_target_pairs={{0,4},{4,0},{8,12},{12,8},{16,20},{20,16},{24,28},{28,24},{1,5},{5... | collective-permute-start | bytes 7077896 | tf_op jit(solution)/shard_map/ppermute | solution.py:56
  273.5 16.3 %collective-permute-start.53 = (bf16[2,2,96,768]{3,2,1,0:T(8,128)(2,1)S(1)}, bf16[2,2,96,768]{3,2,1,0:T(8,128)(2,1)S(1)}, u32[]{:S(2)}, u32[]{:S(2)}) collective-permute-start(bf16[2,2,96,768]{3,2,1,0:T(8,128)(2,1)S(1)} %pad_maximum_fusion.18), channel_id=1, source_target_pairs={{0,8},{4,12},{8,0},{12,4},{16,24},{20,28},{24,16},{28,20},{1,9},{5... | collective-permute-start | bytes 1769480 | tf_op jit(solution)/shard_map/ppermute | solution.py:56
  273.6 16.7 %collective-permute-start.56 = (bf16[2,2,96,768]{3,2,1,0:T(8,128)(2,1)S(1)}, bf16[2,2,96,768]{3,2,1,0:T(8,128)(2,1)S(1)}, u32[]{:S(2)}, u32[]{:S(2)}) collective-permute-start(bf16[2,2,96,768]{3,2,1,0:T(8,128)(2,1)S(1)} %pad_maximum_fusion.19), channel_id=1, source_target_pairs={{0,16},{4,20},{8,24},{12,28},{16,0},{20,4},{24,8},{28,12},{1,17},{... | collective-permute-start | bytes 1769480 | tf_op jit(solution)/shard_map/ppermute | solution.py:56
  274.3 28.1 %collective-permute-start.45 = (bf16[2,2,96,768]{3,2,1,0:T(8,128)(2,1)S(1)}, bf16[2,2,96,768]{3,2,1,0:T(8,128)(2,1)S(1)}, u32[]{:S(2)}, u32[]{:S(2)}) collective-permute-start(bf16[2,2,96,768]{3,2,1,0:T(8,128)(2,1)S(1)} %pad_maximum_fusion.16), channel_id=1, source_target_pairs={{0,8},{4,12},{8,0},{12,4},{16,24},{20,28},{24,16},{28,20},{1,9},{5... | collective-permute-start | bytes 1769480 | tf_op jit(solution)/shard_map/ppermute | solution.py:56
  276.5 26.1 %collective-permute-start.48 = (bf16[2,2,96,768]{3,2,1,0:T(8,128)(2,1)S(1)}, bf16[2,2,96,768]{3,2,1,0:T(8,128)(2,1)S(1)}, u32[]{:S(2)}, u32[]{:S(2)}) collective-permute-start(bf16[2,2,96,768]{3,2,1,0:T(8,128)(2,1)S(1)} %pad_maximum_fusion.17), channel_id=1, source_target_pairs={{0,16},{4,20},{8,24},{12,28},{16,0},{20,4},{24,8},{28,12},{1,17},{... | collective-permute-start | bytes 1769480 | tf_op jit(solution)/shard_map/ppermute | solution.py:56
  280.5 34.6 %collective-permute-start.37 = (bf16[2,2,96,768]{3,2,1,0:T(8,128)(2,1)S(1)}, bf16[2,2,96,768]{3,2,1,0:T(8,128)(2,1)S(1)}, u32[]{:S(2)}, u32[]{:S(2)}) collective-permute-start(bf16[2,2,96,768]{3,2,1,0:T(8,128)(2,1)S(1)} %pad_maximum_fusion.14), channel_id=1, source_target_pairs={{0,8},{4,12},{8,0},{12,4},{16,24},{20,28},{24,16},{28,20},{1,9},{5... | collective-permute-start | bytes 1769480 | tf_op jit(solution)/shard_map/ppermute | solution.py:56
  289.8 25.5 %collective-permute-start.40 = (bf16[2,2,96,768]{3,2,1,0:T(8,128)(2,1)S(1)}, bf16[2,2,96,768]{3,2,1,0:T(8,128)(2,1)S(1)}, u32[]{:S(2)}, u32[]{:S(2)}) collective-permute-start(bf16[2,2,96,768]{3,2,1,0:T(8,128)(2,1)S(1)} %pad_maximum_fusion.15), channel_id=1, source_target_pairs={{0,16},{4,20},{8,24},{12,28},{16,0},{20,4},{24,8},{28,12},{1,17},{... | collective-permute-start | bytes 1769480 | tf_op jit(solution)/shard_map/ppermute | solution.py:56
  290.4 31.2 %collective-permute-start.54 = (bf16[2,96,768]{2,1,0:T(8,128)(2,1)S(1)}, bf16[2,96,768]{2,1,0:T(8,128)(2,1)S(1)}, u32[]{:S(2)}, u32[]{:S(2)}) collective-permute-start(bf16[2,96,768]{2,1,0:T(8,128)(2,1)S(1)} %fusion.127), channel_id=1, source_target_pairs={{0,16},{4,20},{8,24},{12,28},{16,0},{20,4},{24,8},{28,12},{1,17},{... | collective-permute-start | bytes 884744 | tf_op jit(solution)/shard_map/ppermute | solution.py:56
  302.4 21.1 %collective-permute-start.57 = (bf16[2,96,768]{2,1,0:T(8,128)(2,1)S(1)}, bf16[2,96,768]{2,1,0:T(8,128)(2,1)S(1)}, u32[]{:S(2)}, u32[]{:S(2)}) collective-permute-start(bf16[2,96,768]{2,1,0:T(8,128)(2,1)S(1)} %fusion.126), channel_id=1, source_target_pairs={{0,8},{4,12},{8,0},{12,4},{16,24},{20,28},{24,16},{28,20},{1,9},{5... | collective-permute-start | bytes 884744 | tf_op jit(solution)/shard_map/ppermute | solution.py:56
  302.6 25.3 %collective-permute-start.46 = (bf16[2,96,768]{2,1,0:T(8,128)(2,1)S(1)}, bf16[2,96,768]{2,1,0:T(8,128)(2,1)S(1)}, u32[]{:S(2)}, u32[]{:S(2)}) collective-permute-start(bf16[2,96,768]{2,1,0:T(8,128)(2,1)S(1)} %fusion.132), channel_id=1, source_target_pairs={{0,16},{4,20},{8,24},{12,28},{16,0},{20,4},{24,8},{28,12},{1,17},{... | collective-permute-start | bytes 884744 | tf_op jit(solution)/shard_map/ppermute | solution.py:56
  315.1 13.4 %collective-permute-start.49 = (bf16[2,96,768]{2,1,0:T(8,128)(2,1)S(1)}, bf16[2,96,768]{2,1,0:T(8,128)(2,1)S(1)}, u32[]{:S(2)}, u32[]{:S(2)}) collective-permute-start(bf16[2,96,768]{2,1,0:T(8,128)(2,1)S(1)} %fusion.131), channel_id=1, source_target_pairs={{0,8},{4,12},{8,0},{12,4},{16,24},{20,28},{24,16},{28,20},{1,9},{5... | collective-permute-start | bytes 884744 | tf_op jit(solution)/shard_map/ppermute | solution.py:56
  315.2 16.5 %collective-permute-start.38 = (bf16[2,96,768]{2,1,0:T(8,128)(2,1)S(1)}, bf16[2,96,768]{2,1,0:T(8,128)(2,1)S(1)}, u32[]{:S(2)}, u32[]{:S(2)}) collective-permute-start(bf16[2,96,768]{2,1,0:T(8,128)(2,1)S(1)} %fusion.137), channel_id=1, source_target_pairs={{0,16},{4,20},{8,24},{12,28},{16,0},{20,4},{24,8},{28,12},{1,17},{... | collective-permute-start | bytes 884744 | tf_op jit(solution)/shard_map/ppermute | solution.py:56
  327.9 13.3 %collective-permute-start.58 = (bf16[96,768]{1,0:T(8,128)(2,1)S(1)}, bf16[96,768]{1,0:T(8,128)(2,1)S(1)}, u32[]{:S(2)}, u32[]{:S(2)}) collective-permute-start(bf16[96,768]{1,0:T(8,128)(2,1)S(1)} %get-tuple-element.119), channel_id=1, source_target_pairs={{0,2},{1,3},{2,0},{3,1},{4,6},{5,7},{6,4},{7,5},{8,10},{9,11},{10,... | collective-permute-start | bytes 442376 | tf_op jit(solution)/shard_map/ppermute | solution.py:53
  328.5 13.3 %collective-permute-start.55 = (bf16[96,768]{1,0:T(8,128)(2,1)S(1)}, bf16[96,768]{1,0:T(8,128)(2,1)S(1)}, u32[]{:S(2)}, u32[]{:S(2)}) collective-permute-start(bf16[96,768]{1,0:T(8,128)(2,1)S(1)} %slice_bitcast_fusion.39), channel_id=1, source_target_pairs={{0,3},{1,0},{2,1},{3,2},{4,7},{5,4},{6,5},{7,6},{8,11},{9,8},{10,9... | collective-permute-start | bytes 442376 | tf_op jit(solution)/shard_map/ppermute | solution.py:53
  331.8 17.9 %collective-permute-start.51 = (bf16[96,768]{1,0:T(8,128)(2,1)S(1)}, bf16[96,768]{1,0:T(8,128)(2,1)S(1)}, u32[]{:S(2)}, u32[]{:S(2)}) collective-permute-start(bf16[96,768]{1,0:T(8,128)(2,1)S(1)} %get-tuple-element.118), channel_id=1, source_target_pairs={{0,1},{1,2},{2,3},{3,0},{4,5},{5,6},{6,7},{7,4},{8,9},{9,10},{10,1... | collective-permute-start | bytes 442376 | tf_op jit(solution)/shard_map/ppermute | solution.py:53
  331.8 21.6 %collective-permute-start.50 = (bf16[96,768]{1,0:T(8,128)(2,1)S(1)}, bf16[96,768]{1,0:T(8,128)(2,1)S(1)}, u32[]{:S(2)}, u32[]{:S(2)}) collective-permute-start(bf16[96,768]{1,0:T(8,128)(2,1)S(1)} %get-tuple-element.117), channel_id=1, source_target_pairs={{0,2},{1,3},{2,0},{3,1},{4,6},{5,7},{6,4},{7,5},{8,10},{9,11},{10,... | collective-permute-start | bytes 442376 | tf_op jit(solution)/shard_map/ppermute | solution.py:53
  333.7 19.7 %collective-permute-start.47 = (bf16[96,768]{1,0:T(8,128)(2,1)S(1)}, bf16[96,768]{1,0:T(8,128)(2,1)S(1)}, u32[]{:S(2)}, u32[]{:S(2)}) collective-permute-start(bf16[96,768]{1,0:T(8,128)(2,1)S(1)} %slice_bitcast_fusion.43), channel_id=1, source_target_pairs={{0,3},{1,0},{2,1},{3,2},{4,7},{5,4},{6,5},{7,6},{8,11},{9,8},{10,9... | collective-permute-start | bytes 442376 | tf_op jit(solution)/shard_map/ppermute | solution.py:53
  341.8 18.5 %collective-permute-start.42 = (bf16[96,768]{1,0:T(8,128)(2,1)S(1)}, bf16[96,768]{1,0:T(8,128)(2,1)S(1)}, u32[]{:S(2)}, u32[]{:S(2)}) collective-permute-start(bf16[96,768]{1,0:T(8,128)(2,1)S(1)} %get-tuple-element.115), channel_id=1, source_target_pairs={{0,2},{1,3},{2,0},{3,1},{4,6},{5,7},{6,4},{7,5},{8,10},{9,11},{10,... | collective-permute-start | bytes 442376 | tf_op jit(solution)/shard_map/ppermute | solution.py:53
  360.4 16.0 %collective-permute-start.60 = (bf16[288,768]{1,0:T(8,128)(2,1)S(1)}, bf16[288,768]{1,0:T(8,128)(2,1)S(1)}, u32[]{:S(2)}, u32[]{:S(2)}) collective-permute-start(bf16[288,768]{1,0:T(8,128)(2,1)S(1)} %pad_maximum_fusion.20), channel_id=1, source_target_pairs={{0,4},{4,0},{8,12},{12,8},{16,20},{20,16},{24,28},{28,24},{1,5},{5... | collective-permute-start | bytes 1327112 | tf_op jit(solution)/shard_map/ppermute | solution.py:56
  360.5 12.6 %collective-permute-start.61 = (bf16[288,768]{1,0:T(8,128)(2,1)S(1)}, bf16[288,768]{1,0:T(8,128)(2,1)S(1)}, u32[]{:S(2)}, u32[]{:S(2)}) collective-permute-start(bf16[288,768]{1,0:T(8,128)(2,1)S(1)} %pad_maximum_fusion.20), channel_id=1, source_target_pairs={{0,8},{4,12},{8,0},{12,4},{16,24},{20,28},{24,16},{28,20},{1,9},{5... | collective-permute-start | bytes 1327112 | tf_op jit(solution)/shard_map/ppermute | solution.py:56
  360.9 14.6 %collective-permute-start.63 = (bf16[288,768]{1,0:T(8,128)(2,1)S(1)}, bf16[288,768]{1,0:T(8,128)(2,1)S(1)}, u32[]{:S(2)}, u32[]{:S(2)}) collective-permute-start(bf16[288,768]{1,0:T(8,128)(2,1)S(1)} %pad_maximum_fusion.20), channel_id=1, source_target_pairs={{0,16},{4,20},{8,24},{12,28},{16,0},{20,4},{24,8},{28,12},{1,17},{... | collective-permute-start | bytes 1327112 | tf_op jit(solution)/shard_map/ppermute | solution.py:56
  (89 other events, 610.8 us)
